TPU v7x, 32 devices: a whole 2x2x4 slice. The times are simulated.
32 devices in a mesh: grp: 2 (over y), sta: 16 (over z, x, core).
Axes of the slice: x: 2, y: 2, z: 4, core: 2. Of those that a mesh axis runs over, the one named last changes fastest.
Arguments:
- traces: bfloat16 [32, 2048], P(('grp', 'sta')), parts along dimension 0, may hold values from -6 to 6
- templates: bfloat16 [16, 32, 512], P(None, ('grp', 'sta')), parts along dimension 1, may hold values from -6 to 6
- moveouts: int32 [16, 32], P(None, ('grp', 'sta')), parts along dimension 1, may hold values from 0 to 511
- channel_mask: int32 [32], P(('grp', 'sta')), parts along dimension 0, may hold values 0 or 1
- owner_slot: int32 [16], replicated, may hold values from 0 to 15, each once
Outputs:
- updated_templates: bfloat16 [16, 32, 512], P(None, ('grp', 'sta')), parts along dimension 1
- owner_weights: bfloat16 [32, 1024], P(('grp', 'sta')), parts along dimension 0
There are 2 independent parts, one for each index of `grp`. A program takes and returns all parts, laid end to end along the dimension named above; an argument that names none is the same for every part. Nothing has to cross between parts.
Inputs may be any that keep to these rules, and one draw needn't show every extreme that they name: owner_slot names each row of 0 to 15 once.
All inputs are finite; a program needn't handle non-finite values. No bound on the sum of `channel_mask` on one device may be relied on, other than what follows from the above.
Results may differ from a plain program's by a relative error of at most 0.0057.
Values may be sent and summed in bfloat16 or wider, within the bound.
No kernel may reach another device: no remote copies, remote signals or barrier semaphores. Data moves between devices by JAX's collectives and lax.ppermute only.
A program may use at most 64 MiB of HBM per device.

v0:
```python
import functools

import jax
import jax.numpy as jnp
from jax import lax
from jax.experimental import pallas as pl
from jax.experimental.pallas import tpu as pltpu
from jax.sharding import PartitionSpec as P

MOVE = 512
LANES = 128


def column(row):
    n = row.shape[1]
    wide = jnp.broadcast_to(row.astype(jnp.float32), (n, n))
    here = lax.broadcasted_iota(jnp.int32, (n, n), 0) == lax.broadcasted_iota(jnp.int32, (n, n), 1)
    return jnp.sum(jnp.where(here, wide, 0.0), axis=1, keepdims=True).astype(jnp.int32)


def blocks_of(value):
    return [value[:, i : i + LANES] for i in range(0, value.shape[1], LANES)]


def hankel(trace):
    win = trace.shape[1]
    base = jnp.broadcast_to(trace.astype(jnp.float32), (8, win))
    row = lax.broadcasted_iota(jnp.int32, (8, win), 0)
    for step in (1, 2, 4):
        base = jnp.where((row & step) != 0, pltpu.roll(base, win - step, 1), base)
    rows = [base] + [pltpu.roll(base, win - step, 1) for step in range(8, LANES, 8)]
    return jnp.concatenate(rows, axis=0).astype(jnp.bfloat16)


def forward_kernel(span, mask_ref, trace_ref, templates_ref, moves_ref, partial_ref, hankel_ref):
    count, length = templates_ref.shape
    hankel_ref[...] = hankel(trace_ref[...])
    widened = templates_ref[...].astype(jnp.float32)
    normed = widened * lax.rsqrt(jnp.sum(widened * widened, axis=1, keepdims=True) + 1e-06)
    pieces = blocks_of(normed.astype(jnp.bfloat16))
    lags = span + MOVE
    wide = lags + length - LANES
    products = jnp.dot(
        jnp.concatenate(pieces, axis=0),
        hankel_ref[:, :wide],
        preferred_element_type=jnp.float32,
    )
    found = []
    for lag in range(0, lags, LANES):
        terms = [
            products[i * count : (i + 1) * count, lag + i * LANES : lag + (i + 1) * LANES]
            for i in range(len(pieces))
        ]
        found.append(functools.reduce(jnp.add, terms))
    moves = jnp.broadcast_to(column(moves_ref[...]), (count, LANES))
    whole, rest = moves // LANES, moves % LANES
    lane = lax.broadcasted_iota(jnp.int32, (count, LANES), 1)
    source = (lane + rest) % LANES
    inside = lane + rest < LANES
    turned = []
    for j in range(span // LANES + 1):
        near = found[j]
        for h in range(1, MOVE // LANES):
            if j + h < len(found):
                near = jnp.where(whole == h, found[j + h], near)
        turned.append(jnp.take_along_axis(near, source, axis=1))
    weight = mask_ref[0].astype(jnp.float32)
    for j in range(span // LANES):
        partial_ref[:, j * LANES : (j + 1) * LANES] = (
            jnp.where(inside, turned[j], turned[j + 1]) * weight
        )
    partial_ref[:, span:] = jnp.full((count, LANES), weight, jnp.float32)


def adjoint_kernel(
    span, owned, mask_ref, total_ref, hankel_ref, templates_ref, moves_ref, slots_ref,
    updated_ref, own_ref, spread,
):
    count, length = templates_ref.shape
    usable = jnp.max(total_ref[:, span:], axis=1, keepdims=True)
    stack = total_ref[:, :span] * lax.rsqrt(jnp.maximum(usable, 1.0))
    weights = (stack * stack * stack).astype(jnp.bfloat16)
    wide = weights.astype(jnp.float32)
    slots = jnp.broadcast_to(column(slots_ref[...]), (count, span))
    first = lax.axis_index("sta") * owned
    for j in range(owned):
        mine = jnp.sum(jnp.where(slots == first + j, wide, 0.0), axis=0, keepdims=True)
        own_ref[j : j + 1, :] = mine.astype(jnp.bfloat16)
    moves = jnp.broadcast_to(column(moves_ref[...]), (count, LANES))
    whole, rest = moves // LANES, moves % LANES
    lane = lax.broadcasted_iota(jnp.int32, (count, LANES), 1)
    source = (lane + LANES - rest) % LANES
    inside = lane >= rest
    zero = jnp.zeros((count, LANES), jnp.float32)
    turned = [zero] + [jnp.take_along_axis(b, source, axis=1) for b in blocks_of(wide)] + [zero]
    shifted = [jnp.where(inside, turned[j + 1], turned[j]) for j in range(len(turned) - 1)]
    placed = []
    for j in range((span + MOVE) // LANES):
        value = zero
        for h in range(MOVE // LANES):
            if 0 <= j - h < len(shifted):
                value = jnp.where(whole == h, shifted[j - h], value)
        placed.append(value.astype(jnp.bfloat16))
    pieces = length // LANES
    blank = zero.astype(jnp.bfloat16)
    for i in range(pieces):
        for j in range(len(placed) + pieces - 1):
            value = placed[j - i] if 0 <= j - i < len(placed) else blank
            spread[i * count : (i + 1) * count, j * LANES : (j + 1) * LANES] = value
    products = lax.dot_general(
        spread[...],
        hankel_ref[:, : spread.shape[1]],
        (((1,), (1,)), ((), ())),
        preferred_element_type=jnp.float32,
    )
    update = jnp.concatenate(
        [products[i * count : (i + 1) * count] for i in range(pieces)], axis=1
    )
    normal = update * lax.rsqrt(jnp.mean(update * update, axis=1, keepdims=True) + 1e-06)
    usable_here = jnp.broadcast_to(mask_ref[0], (count, length)) == 1
    initial = templates_ref[...].astype(jnp.float32)
    updated_ref[...] = jnp.where(usable_here, normal, initial).astype(jnp.bfloat16)


def body(traces, templates, moveouts, channel_mask, owner_slot):
    count, _, length = templates.shape
    win = traces.shape[1]
    span = win - MOVE - length
    stations = lax.axis_size("sta")
    owned = count // stations
    own_templates = templates.reshape(count, length)
    moves = moveouts.reshape(1, count)
    slots = owner_slot.reshape(1, count)
    scalar = pl.BlockSpec(memory_space=pltpu.SMEM)
    vector = pl.BlockSpec(memory_space=pltpu.VMEM)
    total, lagged = pl.pallas_call(
        functools.partial(forward_kernel, span),
        out_shape=(
            jax.ShapeDtypeStruct((count, span + LANES), jnp.float32),
            jax.ShapeDtypeStruct((LANES, win), jnp.bfloat16),
        ),
        in_specs=[scalar, vector, vector, vector],
        out_specs=(vector, vector),
        name="forward",
    )(channel_mask, traces, own_templates, moves)
    step = 1
    while step < stations:
        pairs = [(i, i ^ step) for i in range(stations)]
        total = total + lax.ppermute(total, "sta", pairs)
        step *= 2
    updated, own = pl.pallas_call(
        functools.partial(adjoint_kernel, span, owned),
        out_shape=(
            jax.ShapeDtypeStruct((count, length), jnp.bfloat16),
            jax.ShapeDtypeStruct((owned, span), jnp.bfloat16),
        ),
        in_specs=[scalar] + [vector] * 5,
        out_specs=(vector, vector),
        scratch_shapes=[
            pltpu.VMEM((count * length // LANES, win - LANES), jnp.bfloat16),
        ],
        name="adjoint",
    )(channel_mask, total, lagged, own_templates, moves, slots)
    return (updated.reshape(count, 1, length), own)


def solution(mesh):
    placed = (
        P(("grp", "sta"), None),
        P(None, ("grp", "sta"), None),
        P(None, ("grp", "sta")),
        P(("grp", "sta")),
        P(),
    )
    return jax.shard_map(
        body,
        mesh=mesh,
        in_specs=placed,
        out_specs=(P(None, ("grp", "sta"), None), P(("grp", "sta"), None)),
        check_vma=False,
    )
```

profile of v0, /device:TPU:0, one launch (start us, length us, event | category | flops | bytes accessed | tf_op | source)
XLA Modules:
  0.0 23.9 jit_solution(12895691256198089616)
XLA Ops:
  1.3 2.0 %forward.1 = (f32[16,1152]{1,0:T(8,128)}, bf16[128,2048]{1,0:T(8,128)(2,1)}) custom-call(s32[1]{0:T(128)S(6)} %copy.7.mask_ref, bf16[1,2048]{1,0:T(2,128)(2,1)} %trace_ref.1, bf16[16,512]{1,0:T(8,128)(2,1)} %bitcast.4, s32[1,16]{1,0:T(1,128)} %bitcast.6), custom_call_target="tpu_custom_call" | custom-call | tf_op jit(solution)/shard_map/forward/pallas_call | solution.py:136
  3.3 0.5 %collective-permute-start = (f32[16,1152]{1,0:T(8,128)}, f32[16,1152]{1,0:T(8,128)S(1)}, u32[]{:S(2)}, u32[]{:S(2)}) collective-permute-start(f32[16,1152]{1,0:T(8,128)} %get-tuple-element.6), channel_id=1, source_target_pairs={{0,1},{1,0},{2,3},{3,2},{4,5},{5,4},{6,7},{7,6},{8,9},{9,8},{10,11... | collective-permute-start | bytes 221192 | tf_op jit(solution)/shard_map/ppermute | solution.py:149
  3.8 1.1 %collective-permute-done = f32[16,1152]{1,0:T(8,128)S(1)} collective-permute-done((f32[16,1152]{1,0:T(8,128)}, f32[16,1152]{1,0:T(8,128)S(1)}, u32[]{:S(2)}, u32[]{:S(2)}) %collective-permute-start) | collective-permute-done | bytes 73760 | tf_op jit(solution)/shard_map/ppermute | solution.py:149
  4.9 0.9 %add.12 = f32[16,1152]{1,0:T(8,128)S(1)} add(f32[16,1152]{1,0:T(8,128)} %get-tuple-element.6, f32[16,1152]{1,0:T(8,128)S(1)} %collective-permute-done) | non-fusion elementwise | flops 18432 | bytes 221184 | tf_op jit(solution)/shard_map/add | solution.py:149
  5.8 2.9 %collective-permute-start.1 = (f32[16,1152]{1,0:T(8,128)S(1)}, f32[16,1152]{1,0:T(8,128)S(1)}, u32[]{:S(2)}, u32[]{:S(2)}) collective-permute-start(f32[16,1152]{1,0:T(8,128)S(1)} %add.12), channel_id=1, source_target_pairs={{0,2},{1,3},{2,0},{3,1},{4,6},{5,7},{6,4},{7,5},{8,10},{9,11},{10,... | collective-permute-start | bytes 221192 | tf_op jit(solution)/shard_map/ppermute | solution.py:149
  8.7 2.6 %collective-permute-done.1 = f32[16,1152]{1,0:T(8,128)S(1)} collective-permute-done((f32[16,1152]{1,0:T(8,128)S(1)}, f32[16,1152]{1,0:T(8,128)S(1)}, u32[]{:S(2)}, u32[]{:S(2)}) %collective-permute-start.1) | collective-permute-done | bytes 73760 | tf_op jit(solution)/shard_map/ppermute | solution.py:149
  11.3 1.9 %collective-permute-start.2 = (f32[16,1152]{1,0:T(8,128)S(1)}, f32[16,1152]{1,0:T(8,128)S(1)}, u32[]{:S(2)}, u32[]{:S(2)}) collective-permute-start(f32[16,1152]{1,0:T(8,128)S(1)} %add.13), channel_id=1, source_target_pairs={{0,4},{1,5},{2,6},{3,7},{4,0},{5,1},{6,2},{7,3},{8,12},{9,13},{10,... | collective-permute-start | bytes 221192 | tf_op jit(solution)/shard_map/ppermute | solution.py:149
  13.2 2.5 %collective-permute-done.2 = f32[16,1152]{1,0:T(8,128)S(1)} collective-permute-done((f32[16,1152]{1,0:T(8,128)S(1)}, f32[16,1152]{1,0:T(8,128)S(1)}, u32[]{:S(2)}, u32[]{:S(2)}) %collective-permute-start.2) | collective-permute-done | bytes 73760 | tf_op jit(solution)/shard_map/ppermute | solution.py:149
  15.7 2.9 %collective-permute-start.3 = (f32[16,1152]{1,0:T(8,128)S(1)}, f32[16,1152]{1,0:T(8,128)S(1)}, u32[]{:S(2)}, u32[]{:S(2)}) collective-permute-start(f32[16,1152]{1,0:T(8,128)S(1)} %add.14), channel_id=1, source_target_pairs={{0,8},{1,9},{2,10},{3,11},{4,12},{5,13},{6,14},{7,15},{8,0},{9,1},... | collective-permute-start | bytes 221192 | tf_op jit(solution)/shard_map/ppermute | solution.py:149
  18.6 2.4 %collective-permute-done.3 = f32[16,1152]{1,0:T(8,128)S(1)} collective-permute-done((f32[16,1152]{1,0:T(8,128)S(1)}, f32[16,1152]{1,0:T(8,128)S(1)}, u32[]{:S(2)}, u32[]{:S(2)}) %collective-permute-start.3) | collective-permute-done | bytes 73760 | tf_op jit(solution)/shard_map/ppermute | solution.py:149
  21.0 0.6 %add.15.total_ref = f32[16,1152]{1,0:T(8,128)} add(f32[16,1152]{1,0:T(8,128)S(1)} %add.14, f32[16,1152]{1,0:T(8,128)S(1)} %collective-permute-done.3) | non-fusion elementwise | flops 18432 | bytes 221184 | tf_op jit(solution)/shard_map/add | solution.py:149
  21.7 2.2 %adjoint.1 = (bf16[16,512]{1,0:T(8,128)(2,1)}, bf16[1,1024]{1,0:T(2,128)(2,1)}) custom-call(s32[1]{0:T(128)S(6)} %copy.7.mask_ref, f32[16,1152]{1,0:T(8,128)} %add.15.total_ref, bf16[128,2048]{1,0:T(8,128)(2,1)} %get-tuple-element.7.hankel_ref, bf16[16,512]{1,0:T(8,128)(2,1)} %bitcast.5, s32[1,16]{1,0:T(1,128)} %bitcast.7, s32[1,16]{1,0:T(1,128)} %bitcast.8), custom_call_target="tpu_custom_call" | custom-call | tf_op jit(solution)/shard_map/adjoint/pallas_call | solution.py:151
  (2 shorter events, 0.0 us)
Async XLA Ops:
  3.3 1.6 %collective-permute-start = (f32[16,1152]{1,0:T(8,128)}, f32[16,1152]{1,0:T(8,128)S(1)}, u32[]{:S(2)}, u32[]{:S(2)}) collective-permute-start(f32[16,1152]{1,0:T(8,128)} %get-tuple-element.6), channel_id=1, source_target_pairs={{0,1},{1,0},{2,3},{3,2},{4,5},{5,4},{6,7},{7,6},{8,9},{9,8},{10,11... | collective-permute-start | bytes 221192 | tf_op jit(solution)/shard_map/ppermute | solution.py:149
  5.8 5.5 %collective-permute-start.1 = (f32[16,1152]{1,0:T(8,128)S(1)}, f32[16,1152]{1,0:T(8,128)S(1)}, u32[]{:S(2)}, u32[]{:S(2)}) collective-permute-start(f32[16,1152]{1,0:T(8,128)S(1)} %add.12), channel_id=1, source_target_pairs={{0,2},{1,3},{2,0},{3,1},{4,6},{5,7},{6,4},{7,5},{8,10},{9,11},{10,... | collective-permute-start | bytes 221192 | tf_op jit(solution)/shard_map/ppermute | solution.py:149
  11.3 4.4 %collective-permute-start.2 = (f32[16,1152]{1,0:T(8,128)S(1)}, f32[16,1152]{1,0:T(8,128)S(1)}, u32[]{:S(2)}, u32[]{:S(2)}) collective-permute-start(f32[16,1152]{1,0:T(8,128)S(1)} %add.13), channel_id=1, source_target_pairs={{0,4},{1,5},{2,6},{3,7},{4,0},{5,1},{6,2},{7,3},{8,12},{9,13},{10,... | collective-permute-start | bytes 221192 | tf_op jit(solution)/shard_map/ppermute | solution.py:149
  15.7 5.3 %collective-permute-start.3 = (f32[16,1152]{1,0:T(8,128)S(1)}, f32[16,1152]{1,0:T(8,128)S(1)}, u32[]{:S(2)}, u32[]{:S(2)}) collective-permute-start(f32[16,1152]{1,0:T(8,128)S(1)} %add.14), channel_id=1, source_target_pairs={{0,8},{1,9},{2,10},{3,11},{4,12},{5,13},{6,14},{7,15},{8,0},{9,1},... | collective-permute-start | bytes 221192 | tf_op jit(solution)/shard_map/ppermute | solution.py:149
where the time goes:
time: 24.2 us; the launch traced here: 23.9 us
  waiting for transfers between devices  8.61 us (36%)
  starting transfers between devices  8.23 us (34%)
  Pallas kernels  4.22 us (17%)
  other arithmetic  1.55 us (6%)
  between operations  1.29 us (5%)
    ppermute x4, waiting for transfers between devices, body(): total = total + lax.ppermute(total, 'sta', pairs)  8.61 us
    ppermute x4, starting transfers between devices, body(): total = total + lax.ppermute(total, 'sta', pairs)  8.23 us
    pallas_call x1, Pallas kernels, body(): pl.pallas_call(functools.partial(adjoint_kernel, span, owned), out_shape=...  2.22 us
    pallas_call x1, Pallas kernels, body(): pl.pallas_call(functools.partial(forward_kernel, span), out_shape=(jax.Sh...  2 us
    add x4, other arithmetic, body(): total = total + lax.ppermute(total, 'sta', pairs)  1.55 us
  transfers between devices with their start and end apart: 4, of which 4 were waited for; matrix products, arithmetic and copies ran while one was open for 0% of the time, Pallas kernels for 0%

commit v1 on v0

v1 whole, which is shorter than its diff:
```python
import functools

import jax
import jax.numpy as jnp
from jax import lax
from jax.experimental import pallas as pl
from jax.experimental.pallas import tpu as pltpu
from jax.sharding import PartitionSpec as P

MOVE = 512
LANES = 128


def side(stations):
    index = lax.axis_index("sta")
    parity = index & 1
    for bit in range(1, stations.bit_length() - 1):
        parity = parity ^ ((index >> bit) & 1)
    return parity


def half_of(rows, which):
    half = rows.shape[0] // 2
    return jnp.where(which == 0, rows[:half], rows[half:])


def column(row):
    n = row.shape[1]
    wide = jnp.broadcast_to(row.astype(jnp.float32), (n, n))
    here = lax.broadcasted_iota(jnp.int32, (n, n), 0) == lax.broadcasted_iota(jnp.int32, (n, n), 1)
    return jnp.sum(jnp.where(here, wide, 0.0), axis=1, keepdims=True).astype(jnp.int32)


def blocks_of(value):
    return [value[:, i : i + LANES] for i in range(0, value.shape[1], LANES)]


def hankel(trace):
    win = trace.shape[1]
    base = jnp.broadcast_to(trace.astype(jnp.float32), (8, win))
    row = lax.broadcasted_iota(jnp.int32, (8, win), 0)
    for step in (1, 2, 4):
        base = jnp.where((row & step) != 0, pltpu.roll(base, win - step, 1), base)
    rows = [base] + [pltpu.roll(base, win - step, 1) for step in range(8, LANES, 8)]
    return jnp.concatenate(rows, axis=0).astype(jnp.bfloat16)


def shifts(moves_ref, which):
    rows = half_of(column(moves_ref[...]), which)
    moves = jnp.broadcast_to(rows, (rows.shape[0], LANES))
    return moves // LANES, moves % LANES


def correlate(span, which, mask_ref, lagged_ref, templates_ref, moves_ref, partial_ref):
    length = templates_ref.shape[1]
    widened = half_of(templates_ref[...].astype(jnp.float32), which)
    count = widened.shape[0]
    normed = widened * lax.rsqrt(jnp.sum(widened * widened, axis=1, keepdims=True) + 1e-06)
    pieces = blocks_of(normed)
    lags = span + MOVE
    products = jnp.dot(
        jnp.concatenate(pieces, axis=0).astype(jnp.bfloat16),
        lagged_ref[:, : lags + length - LANES],
        preferred_element_type=jnp.float32,
    )
    found = []
    for lag in range(0, lags, LANES):
        terms = [
            products[i * count : (i + 1) * count, lag + i * LANES : lag + (i + 1) * LANES]
            for i in range(len(pieces))
        ]
        found.append(functools.reduce(jnp.add, terms))
    whole, rest = shifts(moves_ref, which)
    lane = lax.broadcasted_iota(jnp.int32, (count, LANES), 1)
    source = (lane + rest) % LANES
    inside = lane + rest < LANES
    turned = []
    for j in range(span // LANES + 1):
        near = found[j]
        for h in range(1, MOVE // LANES):
            if j + h < len(found):
                near = jnp.where(whole == h, found[j + h], near)
        turned.append(jnp.take_along_axis(near, source, axis=1))
    weight = mask_ref[0].astype(jnp.float32)
    for j in range(span // LANES):
        partial_ref[:, j * LANES : (j + 1) * LANES] = (
            jnp.where(inside, turned[j], turned[j + 1]) * weight
        )
    partial_ref[:, span:] = jnp.full((count, LANES), weight, jnp.float32)


def sent_kernel(
    span, stations, mask_ref, trace_ref, templates_ref, moves_ref, slots_ref, partial_ref,
    lagged_ref, moves_out, slots_out,
):
    moves_out[...] = moves_ref[...]
    slots_out[...] = slots_ref[...]
    lagged_ref[...] = hankel(trace_ref[...])
    other = 1 - side(stations)
    correlate(span, other, mask_ref, lagged_ref, templates_ref, moves_ref, partial_ref)


def kept_kernel(span, stations, mask_ref, lagged_ref, templates_ref, moves_ref, partial_ref):
    own = side(stations)
    correlate(span, own, mask_ref, lagged_ref, templates_ref, moves_ref, partial_ref)


def cube_kernel(span, held_ref, got_ref, weights_ref):
    total = held_ref[...] + got_ref[...]
    stack = total[:, :span] * lax.rsqrt(jnp.maximum(total[:, span : span + 1], 1.0))
    weights_ref[...] = (stack * stack * stack).astype(jnp.bfloat16)


def adjoint(which, weights, mask_ref, lagged_ref, templates_ref, moves_ref, spread):
    length = templates_ref.shape[1]
    count, span = weights.shape
    whole, rest = shifts(moves_ref, which)
    lane = lax.broadcasted_iota(jnp.int32, (count, LANES), 1)
    source = (lane + LANES - rest) % LANES
    inside = lane >= rest
    zero = jnp.zeros((count, LANES), jnp.float32)
    turned = [jnp.take_along_axis(block, source, axis=1) for block in blocks_of(weights)]
    turned = [zero] + turned + [zero]
    shifted = [jnp.where(inside, turned[j + 1], turned[j]) for j in range(len(turned) - 1)]
    placed = []
    for j in range((span + MOVE) // LANES):
        value = zero
        for h in range(MOVE // LANES):
            if 0 <= j - h < len(shifted):
                value = jnp.where(whole == h, shifted[j - h], value)
        placed.append(value)
    pieces = length // LANES
    for j in range(len(placed) + pieces - 1):
        value = [placed[j - i] if 0 <= j - i < len(placed) else zero for i in range(pieces)]
        spread[:, j * LANES : (j + 1) * LANES] = jnp.concatenate(value, axis=0).astype(jnp.bfloat16)
    products = lax.dot_general(
        spread[...],
        lagged_ref[:, : spread.shape[1]],
        (((1,), (1,)), ((), ())),
        preferred_element_type=jnp.float32,
    )
    update = jnp.concatenate(
        [products[i * count : (i + 1) * count] for i in range(pieces)], axis=1
    )
    normal = update * lax.rsqrt(jnp.mean(update * update, axis=1, keepdims=True) + 1e-06)
    initial = half_of(templates_ref[...].astype(jnp.float32), which)
    return jnp.where(jnp.broadcast_to(mask_ref[0], normal.shape) == 1, normal, initial)


def owned_rows(owned, slots_ref, which, rows):
    slots = jnp.broadcast_to(half_of(column(slots_ref[...]), which), rows.shape)
    first = lax.axis_index("sta") * owned
    found = [
        jnp.sum(jnp.where(slots == first + j, rows, 0.0), axis=0, keepdims=True)
        for j in range(owned)
    ]
    return jnp.concatenate(found, axis=0)


def own_kernel(
    stations, owned, mask_ref, weights_ref, lagged_ref, templates_ref, moves_ref, slots_ref,
    updated_ref, own_ref, spread,
):
    wide = weights_ref[...].astype(jnp.float32)
    which = side(stations)
    updated_ref[...] = adjoint(
        which, wide, mask_ref, lagged_ref, templates_ref, moves_ref, spread
    )
    own_ref[...] = owned_rows(owned, slots_ref, which, wide)


def other_kernel(
    stations, owned, mask_ref, others_ref, ready_ref, found_ref, lagged_ref, templates_ref,
    moves_ref, slots_ref, updated_ref, own_ref, spread,
):
    which = side(stations)
    others = others_ref[...].astype(jnp.float32)
    ready = ready_ref[...]
    rows = found_ref[...] + owned_rows(owned, slots_ref, 1 - which, others)
    own_ref[...] = rows.astype(jnp.bfloat16)
    late = adjoint(1 - which, others, mask_ref, lagged_ref, templates_ref, moves_ref, spread)
    low = jnp.where(which == 0, ready, late)
    high = jnp.where(which == 0, late, ready)
    updated_ref[...] = jnp.concatenate([low, high], axis=0).astype(jnp.bfloat16)


def exchange(rows, step):
    stations = lax.axis_size("sta")
    return lax.ppermute(rows, "sta", [(i, i ^ step) for i in range(stations)])


def body(traces, templates, moveouts, channel_mask, owner_slot):
    count, _, length = templates.shape
    half = count // 2
    win = traces.shape[1]
    span = win - MOVE - length
    stations = lax.axis_size("sta")
    owned = count // stations
    own_templates = templates.reshape(count, length)
    moves = moveouts.reshape(1, count)
    slots = owner_slot.reshape(1, count)
    scalar = pl.BlockSpec(memory_space=pltpu.SMEM)
    vector = pl.BlockSpec(memory_space=pltpu.VMEM)
    near = functools.partial(pltpu.with_memory_space_constraint, memory_space=pltpu.VMEM)
    spread = [pltpu.VMEM((half * length // LANES, win - LANES), jnp.bfloat16)]
    work = pl.CostEstimate(
        flops=2 * count * length * win, bytes_accessed=LANES * win * 8, transcendentals=0
    )
    sent, lagged, near_moves, near_slots = pl.pallas_call(
        functools.partial(sent_kernel, span, stations),
        out_shape=(
            pltpu.VMEM((half, span + LANES), jnp.float32),
            pltpu.VMEM((LANES, win), jnp.bfloat16),
            pltpu.VMEM((1, count), jnp.int32),
            pltpu.VMEM((1, count), jnp.int32),
        ),
        in_specs=[scalar] + [vector] * 4,
        out_specs=(vector,) * 4,
        name="correlate_sent",
    )(channel_mask, traces, own_templates, moves, slots)
    kept = pl.pallas_call(
        functools.partial(kept_kernel, span, stations),
        out_shape=pltpu.VMEM((half, span + LANES), jnp.float32),
        in_specs=[scalar] + [vector] * 3,
        out_specs=vector,
        cost_estimate=work,
        name="correlate_kept",
    )(channel_mask, near(lagged), near(own_templates), near(near_moves))
    held, got = kept, exchange(sent, 1)
    steps = [1 << i for i in range(1, stations.bit_length() - 1)]
    for i in range(0, len(steps), 2):
        held = held + got
        pair = steps[i : i + 2]
        others = [step | 1 for step in pair] + [pair[0] | pair[-1]] * (len(pair) - 1)
        got = functools.reduce(jnp.add, [exchange(held, step) for step in others])
    weights = pl.pallas_call(
        functools.partial(cube_kernel, span),
        out_shape=pltpu.VMEM((half, span), jnp.bfloat16),
        in_specs=[vector] * 2,
        out_specs=vector,
        name="cube",
    )(near(held), near(got))
    ready, found = pl.pallas_call(
        functools.partial(own_kernel, stations, owned),
        out_shape=(
            pltpu.VMEM((half, length), jnp.float32),
            pltpu.VMEM((owned, span), jnp.float32),
        ),
        in_specs=[scalar] + [vector] * 5,
        out_specs=(vector, vector),
        scratch_shapes=spread,
        cost_estimate=work,
        name="adjoint_own",
    )(channel_mask, near(weights), near(lagged), near(own_templates), near(near_moves), near(near_slots))
    updated, own = pl.pallas_call(
        functools.partial(other_kernel, stations, owned),
        out_shape=(
            jax.ShapeDtypeStruct((count, length), jnp.bfloat16),
            jax.ShapeDtypeStruct((owned, span), jnp.bfloat16),
        ),
        in_specs=[scalar] + [vector] * 7,
        out_specs=(vector, vector),
        scratch_shapes=spread,
        name="adjoint_other",
    )(
        channel_mask, near(exchange(weights, 1)), near(ready), near(found), near(lagged),
        near(own_templates), near(near_moves), near(near_slots),
    )
    return (updated.reshape(count, 1, length), own)


def solution(mesh):
    placed = (
        P(("grp", "sta"), None),
        P(None, ("grp", "sta"), None),
        P(None, ("grp", "sta")),
        P(("grp", "sta")),
        P(),
    )
    return jax.shard_map(
        body,
        mesh=mesh,
        in_specs=placed,
        out_specs=(P(None, ("grp", "sta"), None), P(("grp", "sta"), None)),
        check_vma=False,
    )
```

time: 24.2 us -> 18.7 us (0.77)
  waiting for transfers between devices: 8.61 us -> 6.14 us
  other arithmetic: 1.55 us -> 0.02 us
  starting transfers between devices: 8.23 us -> 7.49 us
  Pallas kernels: 4.22 us -> 3.52 us
    ppermute x4 -> x6, waiting for transfers between devices: 8.61 us -> 6.14 us  [exchange(): return lax.ppermute(rows, 'sta', [(i, i ^ step) for i in range(stations)])]
    add x4 -> x2, other arithmetic: 1.55 us -> 0.02 us  [body(): held = held + got]
    ppermute x4 -> x6, starting transfers between devices: 8.23 us -> 7.49 us  [exchange(): return lax.ppermute(rows, 'sta', [(i, i ^ step) for i in range(stations)])]
    pallas_call x2 -> x5, Pallas kernels: 4.22 us -> 3.52 us  [the longest x1 1.43 us: body(): pl.pallas_call(functools.partial(sent_kernel, span, stations), out_shape=...]
  transfers between devices with their start and end apart: 4 -> 6, of which waited for: 4 -> 5; matrix products, arithmetic and copies ran while one was open for 0% -> 0% of each run, Pallas kernels for 0% -> 5%
where the time goes in v1:
time: 18.7 us; the launch traced here: 18.5 us
  starting transfers between devices  7.49 us (40%)
  waiting for transfers between devices  6.14 us (33%)
  Pallas kernels  3.52 us (19%)
  between operations  1.3 us (7%)
    ppermute x6, starting transfers between devices, exchange(): return lax.ppermute(rows, 'sta', [(i, i ^ step) for i in range(stations)])  7.49 us
    ppermute x6, waiting for transfers between devices, exchange(): return lax.ppermute(rows, 'sta', [(i, i ^ step) for i in range(stations)])  6.14 us
    pallas_call x1, Pallas kernels, body(): pl.pallas_call(functools.partial(sent_kernel, span, stations), out_shape=...  1.43 us
    pallas_call x1, Pallas kernels, body(): pl.pallas_call(functools.partial(other_kernel, stations, owned), out_shap...  1.14 us
    pallas_call x1, Pallas kernels, body(): pl.pallas_call(functools.partial(own_kernel, stations, owned), out_shape=...  0.52 us
  transfers between devices with their start and end apart: 6, of which 5 were waited for; matrix products, arithmetic and copies ran while one was open for 0% of the time, Pallas kernels for 5%

profile of v1, /device:TPU:0, one launch (start us, length us, event | category | flops | bytes accessed | tf_op | source)
XLA Modules:
  0.0 18.5 jit_solution(17757898462104980247)
XLA Ops:
  1.3 0.0 copy-start
  1.3 1.4 %correlate_sent.1 = (f32[8,1152]{1,0:T(8,128)S(1)}, bf16[128,2048]{1,0:T(8,128)(2,1)S(1)}, s32[1,16]{1,0:T(1,128)S(1)}, s32[1,16]{1,0:T(1,128)S(1)}) custom-call(s32[1]{0:T(128)S(6)} %copy.7.mask_ref, bf16[1,2048]{1,0:T(2,128)(2,1)} %trace_ref.1, bf16[16,512]{1,0:T(8,128)(2,1)} %bitcast.4, s32[1,16]{1,0:T(1,128)} %bitcast.8, s32[1,16]{1,0:T(1,128)} %bitcast.9), custom_call_target="tpu_custom_call" | custom-call | tf_op jit(solution)/shard_map/correlate_sent/pallas_call | solution.py:209
  2.7 0.6 %collective-permute-start = (f32[8,1152]{1,0:T(8,128)S(1)}, f32[8,1152]{1,0:T(8,128)S(1)}, u32[]{:S(2)}, u32[]{:S(2)}) collective-permute-start(f32[8,1152]{1,0:T(8,128)S(1)} %get-tuple-element.12), channel_id=1, source_target_pairs={{0,1},{1,0},{2,3},{3,2},{4,5},{5,4},{6,7},{7,6},{8,9},{9,8},{10,11... | collective-permute-start | bytes 110600 | tf_op jit(solution)/shard_map/ppermute | solution.py:189
  3.3 0.0 copy-done
  3.3 0.4 %correlate_kept.1 = f32[8,1152]{1,0:T(8,128)S(1)} custom-call(s32[1]{0:T(128)S(6)} %copy.7.mask_ref, bf16[128,2048]{1,0:T(8,128)(2,1)S(1)} %get-tuple-element.10.lagged_ref, bf16[16,512]{1,0:T(8,128)(2,1)S(1)} %bitcast.5, s32[1,16]{1,0:T(1,128)S(1)} %get-tuple-element.11.moves_ref), custom_call_target="tpu_custom_call" | custom-call | flops 33554432 | bytes 2097152 | tf_op jit(solution)/shard_map/correlate_kept/pallas_call | solution.py:221
  3.6 0.5 %collective-permute-done = f32[8,1152]{1,0:T(8,128)S(1)} collective-permute-done((f32[8,1152]{1,0:T(8,128)S(1)}, f32[8,1152]{1,0:T(8,128)S(1)}, u32[]{:S(2)}, u32[]{:S(2)}) %collective-permute-start) | collective-permute-done | bytes 36896 | tf_op jit(solution)/shard_map/ppermute | solution.py:189
  4.1 3.8 %collective-permute-start.3 = (f32[8,1152]{1,0:T(8,128)S(1)}, f32[8,1152]{1,0:T(8,128)S(1)}, u32[]{:S(2)}, u32[]{:S(2)}) collective-permute-start(f32[8,1152]{1,0:T(8,128)S(1)} %add.12), channel_id=1, source_target_pairs={{0,6},{1,7},{2,4},{3,5},{4,2},{5,3},{6,0},{7,1},{8,14},{9,15},{10,... | collective-permute-start | bytes 110600 | tf_op jit(solution)/shard_map/ppermute | solution.py:189
  8.0 0.0 collective-permute-start.2
  8.0 0.4 %collective-permute-start.1 = (f32[8,1152]{1,0:T(8,128)S(1)}, f32[8,1152]{1,0:T(8,128)S(1)}, u32[]{:S(2)}, u32[]{:S(2)}) collective-permute-start(f32[8,1152]{1,0:T(8,128)S(1)} %add.12), channel_id=1, source_target_pairs={{0,3},{1,2},{2,1},{3,0},{4,7},{5,6},{6,5},{7,4},{8,11},{9,10},{10,... | collective-permute-start | bytes 110600 | tf_op jit(solution)/shard_map/ppermute | solution.py:189
  8.3 1.6 %collective-permute-done.3 = f32[8,1152]{1,0:T(8,128)S(1)} collective-permute-done((f32[8,1152]{1,0:T(8,128)S(1)}, f32[8,1152]{1,0:T(8,128)S(1)}, u32[]{:S(2)}, u32[]{:S(2)}) %collective-permute-start.3) | collective-permute-done | bytes 36896 | tf_op jit(solution)/shard_map/ppermute | solution.py:189
  9.9 1.8 %collective-permute-done.2 = f32[8,1152]{1,0:T(8,128)S(1)} collective-permute-done((f32[8,1152]{1,0:T(8,128)S(1)}, f32[8,1152]{1,0:T(8,128)S(1)}, u32[]{:S(2)}, u32[]{:S(2)}) %collective-permute-start.2) | collective-permute-done | bytes 36896 | tf_op jit(solution)/shard_map/ppermute | solution.py:189
  11.7 0.0 collective-permute-done.1
  11.7 2.5 %collective-permute-start.4 = (f32[8,1152]{1,0:T(8,128)S(1)}, f32[8,1152]{1,0:T(8,128)S(1)}, u32[]{:S(2)}, u32[]{:S(2)}) collective-permute-start(f32[8,1152]{1,0:T(8,128)S(1)} %add_add_fusion.held_ref), channel_id=1, source_target_pairs={{0,9},{1,8},{2,11},{3,10},{4,13},{5,12},{6,15},{7,14},{8,1},{9,0},... | collective-permute-start | bytes 110600 | tf_op jit(solution)/shard_map/ppermute | solution.py:189
  14.2 1.9 %collective-permute-done.4.got_ref = f32[8,1152]{1,0:T(8,128)S(1)} collective-permute-done((f32[8,1152]{1,0:T(8,128)S(1)}, f32[8,1152]{1,0:T(8,128)S(1)}, u32[]{:S(2)}, u32[]{:S(2)}) %collective-permute-start.4) | collective-permute-done | bytes 36896 | tf_op jit(solution)/shard_map/ppermute | solution.py:189
  16.1 0.1 cube.1.weights_ref
  16.1 0.2 %collective-permute-start.5 = (bf16[8,1024]{1,0:T(8,128)(2,1)S(1)}, bf16[8,1024]{1,0:T(8,128)(2,1)S(1)}, u32[]{:S(2)}, u32[]{:S(2)}) collective-permute-start(bf16[8,1024]{1,0:T(8,128)(2,1)S(1)} %cube.1.weights_ref), channel_id=1, source_target_pairs={{0,1},{1,0},{2,3},{3,2},{4,5},{5,4},{6,7},{7,6},{8,9},{9,8},{10,11... | collective-permute-start | bytes 49160 | tf_op jit(solution)/shard_map/ppermute | solution.py:189
  16.4 0.5 %adjoint_own.1 = (f32[8,512]{1,0:T(8,128)S(1)}, f32[1,1024]{1,0:T(1,128)S(1)}) custom-call(s32[1]{0:T(128)S(6)} %copy.7.mask_ref, bf16[8,1024]{1,0:T(8,128)(2,1)S(1)} %cube.1.weights_ref, bf16[128,2048]{1,0:T(8,128)(2,1)S(1)} %get-tuple-element.10.lagged_ref, bf16[16,512]{1,0:T(8,128)(2,1)S(1)} %bitcast.6, s32[1,16]{1,0:T(1,128)S(1)} %get-tuple-element.11.moves_ref, ...), custom_call_target="tpu_custom_call" | custom-call | flops 33554432 | bytes 2097152 | tf_op jit(solution)/shard_map/adjoint_own/pallas_call | solution.py:243
  16.9 0.4 %collective-permute-done.5.others_ref = bf16[8,1024]{1,0:T(8,128)(2,1)S(1)} collective-permute-done((bf16[8,1024]{1,0:T(8,128)(2,1)S(1)}, bf16[8,1024]{1,0:T(8,128)(2,1)S(1)}, u32[]{:S(2)}, u32[]{:S(2)}) %collective-permute-start.5) | collective-permute-done | bytes 16416 | tf_op jit(solution)/shard_map/ppermute | solution.py:189
  17.3 1.1 %adjoint_other.1 = (bf16[16,512]{1,0:T(8,128)(2,1)}, bf16[1,1024]{1,0:T(2,128)(2,1)}) custom-call(s32[1]{0:T(128)S(6)} %copy.7.mask_ref, bf16[8,1024]{1,0:T(8,128)(2,1)S(1)} %collective-permute-done.5.others_ref, f32[8,512]{1,0:T(8,128)S(1)} %get-tuple-element.14.ready_ref, f32[1,1024]{1,0:T(1,128)S(1)} %get-tuple-element.15.found_ref, ...), custom_call_target="tpu_custom_call" | custom-call | tf_op jit(solution)/shard_map/adjoint_other/pallas_call | solution.py:255
  (2 shorter events, 0.0 us)
Async XLA Ops:
  1.3 2.0 %copy-start = (bf16[16,1,512]{2,0,1:T(8,128)(2,1)S(1)}, bf16[16,1,512]{2,0,1:T(8,128)(2,1)}, u32[]{:S(2)}) copy-start(bf16[16,1,512]{2,0,1:T(8,128)(2,1)} %param.6) | copy-start | bytes 49156
  2.7 1.4 %collective-permute-start = (f32[8,1152]{1,0:T(8,128)S(1)}, f32[8,1152]{1,0:T(8,128)S(1)}, u32[]{:S(2)}, u32[]{:S(2)}) collective-permute-start(f32[8,1152]{1,0:T(8,128)S(1)} %get-tuple-element.12), channel_id=1, source_target_pairs={{0,1},{1,0},{2,3},{3,2},{4,5},{5,4},{6,7},{7,6},{8,9},{9,8},{10,11... | collective-permute-start | bytes 110600 | tf_op jit(solution)/shard_map/ppermute | solution.py:189
  4.1 5.8 %collective-permute-start.3 = (f32[8,1152]{1,0:T(8,128)S(1)}, f32[8,1152]{1,0:T(8,128)S(1)}, u32[]{:S(2)}, u32[]{:S(2)}) collective-permute-start(f32[8,1152]{1,0:T(8,128)S(1)} %add.12), channel_id=1, source_target_pairs={{0,6},{1,7},{2,4},{3,5},{4,2},{5,3},{6,0},{7,1},{8,14},{9,15},{10,... | collective-permute-start | bytes 110600 | tf_op jit(solution)/shard_map/ppermute | solution.py:189
  8.0 3.7 %collective-permute-start.2 = (f32[8,1152]{1,0:T(8,128)S(1)}, f32[8,1152]{1,0:T(8,128)S(1)}, u32[]{:S(2)}, u32[]{:S(2)}) collective-permute-start(f32[8,1152]{1,0:T(8,128)S(1)} %add.12), channel_id=1, source_target_pairs={{0,5},{1,4},{2,7},{3,6},{4,1},{5,0},{6,3},{7,2},{8,13},{9,12},{10,... | collective-permute-start | bytes 110600 | tf_op jit(solution)/shard_map/ppermute | solution.py:189
  8.0 3.7 %collective-permute-start.1 = (f32[8,1152]{1,0:T(8,128)S(1)}, f32[8,1152]{1,0:T(8,128)S(1)}, u32[]{:S(2)}, u32[]{:S(2)}) collective-permute-start(f32[8,1152]{1,0:T(8,128)S(1)} %add.12), channel_id=1, source_target_pairs={{0,3},{1,2},{2,1},{3,0},{4,7},{5,6},{6,5},{7,4},{8,11},{9,10},{10,... | collective-permute-start | bytes 110600 | tf_op jit(solution)/shard_map/ppermute | solution.py:189
  11.7 4.3 %collective-permute-start.4 = (f32[8,1152]{1,0:T(8,128)S(1)}, f32[8,1152]{1,0:T(8,128)S(1)}, u32[]{:S(2)}, u32[]{:S(2)}) collective-permute-start(f32[8,1152]{1,0:T(8,128)S(1)} %add_add_fusion.held_ref), channel_id=1, source_target_pairs={{0,9},{1,8},{2,11},{3,10},{4,13},{5,12},{6,15},{7,14},{8,1},{9,0},... | collective-permute-start | bytes 110600 | tf_op jit(solution)/shard_map/ppermute | solution.py:189
  16.1 1.2 %collective-permute-start.5 = (bf16[8,1024]{1,0:T(8,128)(2,1)S(1)}, bf16[8,1024]{1,0:T(8,128)(2,1)S(1)}, u32[]{:S(2)}, u32[]{:S(2)}) collective-permute-start(bf16[8,1024]{1,0:T(8,128)(2,1)S(1)} %cube.1.weights_ref), channel_id=1, source_target_pairs={{0,1},{1,0},{2,3},{3,2},{4,5},{5,4},{6,7},{7,6},{8,9},{9,8},{10,11... | collective-permute-start | bytes 49160 | tf_op jit(solution)/shard_map/ppermute | solution.py:189

commit v2 on v1

--- a/solution.py
+++ b/solution.py
@@ -6,6 +6,7 @@
 from jax.experimental import pallas as pl
 from jax.experimental.pallas import tpu as pltpu
 from jax.sharding import PartitionSpec as P
+
 
 MOVE = 512
 LANES = 128
@@ -51,7 +52,9 @@
     return moves // LANES, moves % LANES
 
 
-def correlate(span, which, mask_ref, lagged_ref, templates_ref, moves_ref, partial_ref):
+def correlate(
+    span, which, mask_ref, lagged_ref, templates_ref, moves_ref, partial_ref, moves_ready=None
+):
     length = templates_ref.shape[1]
     widened = half_of(templates_ref[...].astype(jnp.float32), which)
     count = widened.shape[0]
@@ -70,6 +73,8 @@
             for i in range(len(pieces))
         ]
         found.append(functools.reduce(jnp.add, terms))
+    if moves_ready is not None:
+        moves_ready()
     whole, rest = shifts(moves_ref, which)
     lane = lax.broadcasted_iota(jnp.int32, (count, LANES), 1)
     source = (lane + rest) % LANES
@@ -89,15 +94,29 @@
     partial_ref[:, span:] = jnp.full((count, LANES), weight, jnp.float32)
 
 
+def lead_kernel(lead_ref):
+    lead_ref[...] = jnp.ones_like(lead_ref)
+
+
 def sent_kernel(
-    span, stations, mask_ref, trace_ref, templates_ref, moves_ref, slots_ref, partial_ref,
-    lagged_ref, moves_out, slots_out,
-):
-    moves_out[...] = moves_ref[...]
-    slots_out[...] = slots_ref[...]
+    span, stations, mask_ref, lead_ref, trace_ref, templates_ref, moves_far, slots_far,
+    partial_ref, lagged_ref, moves_ref, slots_ref, arrived,
+):
+    del lead_ref
+    moves_copy = pltpu.make_async_copy(moves_far, moves_ref, arrived.at[0])
+    slots_copy = pltpu.make_async_copy(slots_far, slots_ref, arrived.at[1])
+
+    @pl.when(lax.axis_index("sta") >= 0)
+    def _():
+        moves_copy.start()
+        slots_copy.start()
+
     lagged_ref[...] = hankel(trace_ref[...])
     other = 1 - side(stations)
-    correlate(span, other, mask_ref, lagged_ref, templates_ref, moves_ref, partial_ref)
+    correlate(
+        span, other, mask_ref, lagged_ref, templates_ref, moves_ref, partial_ref, moves_copy.wait
+    )
+    slots_copy.wait()
 
 
 def kept_kernel(span, stations, mask_ref, lagged_ref, templates_ref, moves_ref, partial_ref):
@@ -111,10 +130,25 @@
     weights_ref[...] = (stack * stack * stack).astype(jnp.bfloat16)
 
 
-def adjoint(which, weights, mask_ref, lagged_ref, templates_ref, moves_ref, spread):
-    length = templates_ref.shape[1]
+def prepare_kernel(
+    stations, owned, lagged_ref, templates_ref, moves_ref, slots_ref, turned_ref, whole_ref,
+    rest_ref, slots_out, initial_ref,
+):
+    turned_ref[...] = lagged_ref[...].astype(jnp.float32).T.astype(jnp.bfloat16)
+    own = side(stations)
+    templates = templates_ref[...].astype(jnp.float32)
+    first = lax.axis_index("sta") * owned
+    for place, which in enumerate((own, 1 - own)):
+        whole_ref[place], rest_ref[place] = shifts(moves_ref, which)
+        slots = half_of(column(slots_ref[...]), which) - first
+        slots_out[place] = jnp.broadcast_to(slots, slots_out.shape[1:])
+        initial_ref[place] = half_of(templates, which)
+
+
+def adjoint(place, weights, mask_ref, turned_ref, whole_ref, rest_ref, initial_ref, spread):
     count, span = weights.shape
-    whole, rest = shifts(moves_ref, which)
+    length = initial_ref.shape[2]
+    whole, rest = whole_ref[place], rest_ref[place]
     lane = lax.broadcasted_iota(jnp.int32, (count, LANES), 1)
     source = (lane + LANES - rest) % LANES
     inside = lane >= rest
@@ -133,52 +167,46 @@
     for j in range(len(placed) + pieces - 1):
         value = [placed[j - i] if 0 <= j - i < len(placed) else zero for i in range(pieces)]
         spread[:, j * LANES : (j + 1) * LANES] = jnp.concatenate(value, axis=0).astype(jnp.bfloat16)
-    products = lax.dot_general(
-        spread[...],
-        lagged_ref[:, : spread.shape[1]],
-        (((1,), (1,)), ((), ())),
-        preferred_element_type=jnp.float32,
+    products = jnp.dot(
+        spread[...], turned_ref[: spread.shape[1], :], preferred_element_type=jnp.float32
     )
     update = jnp.concatenate(
         [products[i * count : (i + 1) * count] for i in range(pieces)], axis=1
     )
     normal = update * lax.rsqrt(jnp.mean(update * update, axis=1, keepdims=True) + 1e-06)
-    initial = half_of(templates_ref[...].astype(jnp.float32), which)
-    return jnp.where(jnp.broadcast_to(mask_ref[0], normal.shape) == 1, normal, initial)
-
-
-def owned_rows(owned, slots_ref, which, rows):
-    slots = jnp.broadcast_to(half_of(column(slots_ref[...]), which), rows.shape)
-    first = lax.axis_index("sta") * owned
+    usable = jnp.broadcast_to(mask_ref[0], normal.shape) == 1
+    return jnp.where(usable, normal, initial_ref[place])
+
+
+def owned_rows(owned, place, slots_ref, rows):
+    slots = jnp.tile(slots_ref[place], (1, rows.shape[1] // LANES))
     found = [
-        jnp.sum(jnp.where(slots == first + j, rows, 0.0), axis=0, keepdims=True)
-        for j in range(owned)
+        jnp.sum(jnp.where(slots == j, rows, 0.0), axis=0, keepdims=True) for j in range(owned)
     ]
     return jnp.concatenate(found, axis=0)
 
 
 def own_kernel(
-    stations, owned, mask_ref, weights_ref, lagged_ref, templates_ref, moves_ref, slots_ref,
+    owned, mask_ref, weights_ref, turned_ref, whole_ref, rest_ref, slots_ref, initial_ref,
     updated_ref, own_ref, spread,
 ):
     wide = weights_ref[...].astype(jnp.float32)
-    which = side(stations)
     updated_ref[...] = adjoint(
-        which, wide, mask_ref, lagged_ref, templates_ref, moves_ref, spread
-    )
-    own_ref[...] = owned_rows(owned, slots_ref, which, wide)
+        0, wide, mask_ref, turned_ref, whole_ref, rest_ref, initial_ref, spread
+    )
+    own_ref[...] = owned_rows(owned, 0, slots_ref, wide)
 
 
 def other_kernel(
-    stations, owned, mask_ref, others_ref, ready_ref, found_ref, lagged_ref, templates_ref,
-    moves_ref, slots_ref, updated_ref, own_ref, spread,
+    stations, owned, mask_ref, others_ref, ready_ref, found_ref, turned_ref, whole_ref,
+    rest_ref, slots_ref, initial_ref, updated_ref, own_ref, spread,
 ):
     which = side(stations)
     others = others_ref[...].astype(jnp.float32)
     ready = ready_ref[...]
-    rows = found_ref[...] + owned_rows(owned, slots_ref, 1 - which, others)
+    rows = found_ref[...] + owned_rows(owned, 1, slots_ref, others)
     own_ref[...] = rows.astype(jnp.bfloat16)
-    late = adjoint(1 - which, others, mask_ref, lagged_ref, templates_ref, moves_ref, spread)
+    late = adjoint(1, others, mask_ref, turned_ref, whole_ref, rest_ref, initial_ref, spread)
     low = jnp.where(which == 0, ready, late)
     high = jnp.where(which == 0, late, ready)
     updated_ref[...] = jnp.concatenate([low, high], axis=0).astype(jnp.bfloat16)
@@ -189,7 +217,16 @@
     return lax.ppermute(rows, "sta", [(i, i ^ step) for i in range(stations)])
 
 
-def body(traces, templates, moveouts, channel_mask, owner_slot):
+def stages(stations):
+    bits = [1 << i for i in range(1, stations.bit_length() - 1)]
+    pairs = [bits[i : i + 2] for i in range(0, len(bits), 2)]
+    return [
+        [pair[0] | pair[1], pair[1] | 1, pair[0] | 1] if len(pair) == 2 else [pair[0] | 1]
+        for pair in pairs
+    ]
+
+
+def whole_step(traces, templates, moveouts, channel_mask, owner_slot):
     count, _, length = templates.shape
     half = count // 2
     win = traces.shape[1]
@@ -206,7 +243,17 @@
     work = pl.CostEstimate(
         flops=2 * count * length * win, bytes_accessed=LANES * win * 8, transcendentals=0
     )
-    sent, lagged, near_moves, near_slots = pl.pallas_call(
+    lead = pl.pallas_call(
+        lead_kernel,
+        out_shape=pltpu.VMEM((8, LANES), jnp.float32),
+        out_specs=vector,
+        cost_estimate=pl.CostEstimate(flops=10**9, bytes_accessed=10**7, transcendentals=0),
+        name="lead",
+    )()
+    trace = near(traces)
+    own_templates = near(own_templates)
+    far = pl.BlockSpec(memory_space=pltpu.HBM)
+    sent, lagged, moves, slots = pl.pallas_call(
         functools.partial(sent_kernel, span, stations),
         out_shape=(
             pltpu.VMEM((half, span + LANES), jnp.float32),
@@ -214,10 +261,12 @@
             pltpu.VMEM((1, count), jnp.int32),
             pltpu.VMEM((1, count), jnp.int32),
         ),
-        in_specs=[scalar] + [vector] * 4,
+        in_specs=[scalar] + [vector] * 3 + [far] * 2,
         out_specs=(vector,) * 4,
+        scratch_shapes=[pltpu.SemaphoreType.DMA((2,))],
         name="correlate_sent",
-    )(channel_mask, traces, own_templates, moves, slots)
+    )(channel_mask, near(lead), trace, own_templates, moves, slots)
+    moves, slots = near(moves), near(slots)
     kept = pl.pallas_call(
         functools.partial(kept_kernel, span, stations),
         out_shape=pltpu.VMEM((half, span + LANES), jnp.float32),
@@ -225,14 +274,29 @@
         out_specs=vector,
         cost_estimate=work,
         name="correlate_kept",
-    )(channel_mask, near(lagged), near(own_templates), near(near_moves))
+    )(channel_mask, near(lagged), own_templates, moves)
+    ahead = pl.pallas_call(
+        functools.partial(prepare_kernel, stations, owned),
+        out_shape=(
+            pltpu.VMEM((win, LANES), jnp.bfloat16),
+            pltpu.VMEM((2, half, LANES), jnp.int32),
+            pltpu.VMEM((2, half, LANES), jnp.int32),
+            pltpu.VMEM((2, half, LANES), jnp.int32),
+            pltpu.VMEM((2, half, length), jnp.float32),
+        ),
+        in_specs=[vector] * 4,
+        out_specs=(vector,) * 5,
+        cost_estimate=work,
+        name="prepare",
+    )(near(lagged), own_templates, moves, slots)
+    ahead = [near(value) for value in ahead]
     held, got = kept, exchange(sent, 1)
-    steps = [1 << i for i in range(1, stations.bit_length() - 1)]
-    for i in range(0, len(steps), 2):
+    for hops in stages(stations):
         held = held + got
-        pair = steps[i : i + 2]
-        others = [step | 1 for step in pair] + [pair[0] | pair[-1]] * (len(pair) - 1)
-        got = functools.reduce(jnp.add, [exchange(held, step) for step in others])
+        parts = []
+        for step in hops:
+            parts.append(exchange(held, step))
+        got = functools.reduce(jnp.add, parts)
     weights = pl.pallas_call(
         functools.partial(cube_kernel, span),
         out_shape=pltpu.VMEM((half, span), jnp.bfloat16),
@@ -241,31 +305,28 @@
         name="cube",
     )(near(held), near(got))
     ready, found = pl.pallas_call(
-        functools.partial(own_kernel, stations, owned),
+        functools.partial(own_kernel, owned),
         out_shape=(
             pltpu.VMEM((half, length), jnp.float32),
             pltpu.VMEM((owned, span), jnp.float32),
         ),
-        in_specs=[scalar] + [vector] * 5,
+        in_specs=[scalar] + [vector] * 6,
         out_specs=(vector, vector),
         scratch_shapes=spread,
         cost_estimate=work,
         name="adjoint_own",
-    )(channel_mask, near(weights), near(lagged), near(own_templates), near(near_moves), near(near_slots))
+    )(channel_mask, near(weights), *ahead)
     updated, own = pl.pallas_call(
         functools.partial(other_kernel, stations, owned),
         out_shape=(
             jax.ShapeDtypeStruct((count, length), jnp.bfloat16),
             jax.ShapeDtypeStruct((owned, span), jnp.bfloat16),
         ),
-        in_specs=[scalar] + [vector] * 7,
+        in_specs=[scalar] + [vector] * 8,
         out_specs=(vector, vector),
         scratch_shapes=spread,
         name="adjoint_other",
-    )(
-        channel_mask, near(exchange(weights, 1)), near(ready), near(found), near(lagged),
-        near(own_templates), near(near_moves), near(near_slots),
-    )
+    )(channel_mask, near(exchange(weights, 1)), near(ready), near(found), *ahead)
     return (updated.reshape(count, 1, length), own)
 
 
@@ -278,7 +339,7 @@
         P(),
     )
     return jax.shard_map(
-        body,
+        whole_step,
         mesh=mesh,
         in_specs=placed,
         out_specs=(P(None, ("grp", "sta"), None), P(("grp", "sta"), None)),

time: 18.7 us -> 18.2 us (0.973)
  Pallas kernels: 3.52 us -> 3.02 us
    pallas_call x5 -> x7, Pallas kernels: 3.52 us -> 3.02 us  [the longest x1 1.02 us: whole_step(): pl.pallas_call(functools.partial(sent_kernel, span, stations), out_shape=...]
where the time goes in v2:
time: 18.2 us; the launch traced here: 18 us
  starting transfers between devices  7.49 us (41%)
  waiting for transfers between devices  6.05 us (33%)
  Pallas kernels  3.02 us (17%)
  between operations  1.34 us (7%)
    ppermute x6, starting transfers between devices, exchange(): return lax.ppermute(rows, 'sta', [(i, i ^ step) for i in range(stations)])  7.49 us
    ppermute x6, waiting for transfers between devices, exchange(): return lax.ppermute(rows, 'sta', [(i, i ^ step) for i in range(stations)])  6.05 us
    pallas_call x1, Pallas kernels, whole_step(): pl.pallas_call(functools.partial(sent_kernel, span, stations), out_shape=...  1.02 us
    pallas_call x1, Pallas kernels, whole_step(): pl.pallas_call(functools.partial(other_kernel, stations, owned), out_shap...  0.97 us
  transfers between devices with their start and end apart: 6, of which 5 were waited for; matrix products, arithmetic and copies ran while one was open for 0% of the time, Pallas kernels for 5%

profile of v2, /device:TPU:0, one launch (start us, length us, event | category | flops | bytes accessed | tf_op | source)
XLA Modules:
  0.0 18.0 jit_solution(4167786996966457190)
XLA Ops:
  0.6 0.0 copy-start
  0.6 0.0 copy-start.1
  1.3 0.0 copy-done
  1.3 0.0 copy-done.1
  1.4 1.0 %correlate_sent.1 = (f32[8,1152]{1,0:T(8,128)S(1)}, bf16[128,2048]{1,0:T(8,128)(2,1)S(1)}, s32[1,16]{1,0:T(1,128)S(1)}, s32[1,16]{1,0:T(1,128)S(1)}) custom-call(s32[1]{0:T(128)S(6)} %copy.7.mask_ref, f32[8,128]{1,0:T(8,128)S(1)} %lead.1.lead_ref, bf16[1,2048]{1,0:T(2,128)(2,1)S(1)} %copy-done.1, bf16[16,512]{1,0:T(8,128)(2,1)S(1)} %bitcast.4, ...), custom_call_target="tpu_custom_call" | custom-call | tf_op jit(solution)/shard_map/correlate_sent/pallas_call | solution.py:256
  2.4 0.6 %collective-permute-start = (f32[8,1152]{1,0:T(8,128)S(1)}, f32[8,1152]{1,0:T(8,128)S(1)}, u32[]{:S(2)}, u32[]{:S(2)}) collective-permute-start(f32[8,1152]{1,0:T(8,128)S(1)} %get-tuple-element.17), channel_id=1, source_target_pairs={{0,1},{1,0},{2,3},{3,2},{4,5},{5,4},{6,7},{7,6},{8,9},{9,8},{10,11... | collective-permute-start | bytes 110600 | tf_op jit(solution)/shard_map/ppermute | solution.py:217
  2.9 0.4 %correlate_kept.1 = f32[8,1152]{1,0:T(8,128)S(1)} custom-call(s32[1]{0:T(128)S(6)} %copy.7.mask_ref, bf16[128,2048]{1,0:T(8,128)(2,1)S(1)} %get-tuple-element.15.lagged_ref, bf16[16,512]{1,0:T(8,128)(2,1)S(1)} %bitcast.5, s32[1,16]{1,0:T(1,128)S(1)} %get-tuple-element.16.moves_ref), custom_call_target="tpu_custom_call" | custom-call | flops 33554432 | bytes 2097152 | tf_op jit(solution)/shard_map/correlate_kept/pallas_call | solution.py:270
  3.3 0.5 %collective-permute-done = f32[8,1152]{1,0:T(8,128)S(1)} collective-permute-done((f32[8,1152]{1,0:T(8,128)S(1)}, f32[8,1152]{1,0:T(8,128)S(1)}, u32[]{:S(2)}, u32[]{:S(2)}) %collective-permute-start) | collective-permute-done | bytes 36896 | tf_op jit(solution)/shard_map/ppermute | solution.py:217
  3.8 3.8 %collective-permute-start.1 = (f32[8,1152]{1,0:T(8,128)S(1)}, f32[8,1152]{1,0:T(8,128)S(1)}, u32[]{:S(2)}, u32[]{:S(2)}) collective-permute-start(f32[8,1152]{1,0:T(8,128)S(1)} %add.12), channel_id=1, source_target_pairs={{0,6},{1,7},{2,4},{3,5},{4,2},{5,3},{6,0},{7,1},{8,14},{9,15},{10,... | collective-permute-start | bytes 110600 | tf_op jit(solution)/shard_map/ppermute | solution.py:217
  7.6 0.0 collective-permute-start.2
  7.7 0.4 %collective-permute-start.3 = (f32[8,1152]{1,0:T(8,128)S(1)}, f32[8,1152]{1,0:T(8,128)S(1)}, u32[]{:S(2)}, u32[]{:S(2)}) collective-permute-start(f32[8,1152]{1,0:T(8,128)S(1)} %add.12), channel_id=1, source_target_pairs={{0,3},{1,2},{2,1},{3,0},{4,7},{5,6},{6,5},{7,4},{8,11},{9,10},{10,... | collective-permute-start | bytes 110600 | tf_op jit(solution)/shard_map/ppermute | solution.py:217
  8.0 1.6 %collective-permute-done.1 = f32[8,1152]{1,0:T(8,128)S(1)} collective-permute-done((f32[8,1152]{1,0:T(8,128)S(1)}, f32[8,1152]{1,0:T(8,128)S(1)}, u32[]{:S(2)}, u32[]{:S(2)}) %collective-permute-start.1) | collective-permute-done | bytes 36896 | tf_op jit(solution)/shard_map/ppermute | solution.py:217
  9.6 1.8 %collective-permute-done.2 = f32[8,1152]{1,0:T(8,128)S(1)} collective-permute-done((f32[8,1152]{1,0:T(8,128)S(1)}, f32[8,1152]{1,0:T(8,128)S(1)}, u32[]{:S(2)}, u32[]{:S(2)}) %collective-permute-start.2) | collective-permute-done | bytes 36896 | tf_op jit(solution)/shard_map/ppermute | solution.py:217
  11.4 0.0 collective-permute-done.3
  11.4 2.5 %collective-permute-start.4 = (f32[8,1152]{1,0:T(8,128)S(1)}, f32[8,1152]{1,0:T(8,128)S(1)}, u32[]{:S(2)}, u32[]{:S(2)}) collective-permute-start(f32[8,1152]{1,0:T(8,128)S(1)} %add_add_fusion.held_ref), channel_id=1, source_target_pairs={{0,9},{1,8},{2,11},{3,10},{4,13},{5,12},{6,15},{7,14},{8,1},{9,0},... | collective-permute-start | bytes 110600 | tf_op jit(solution)/shard_map/ppermute | solution.py:217
  13.9 1.9 %collective-permute-done.4.got_ref = f32[8,1152]{1,0:T(8,128)S(1)} collective-permute-done((f32[8,1152]{1,0:T(8,128)S(1)}, f32[8,1152]{1,0:T(8,128)S(1)}, u32[]{:S(2)}, u32[]{:S(2)}) %collective-permute-start.4) | collective-permute-done | bytes 36896 | tf_op jit(solution)/shard_map/ppermute | solution.py:217
  15.7 0.1 cube.1.weights_ref
  15.8 0.2 %collective-permute-start.5 = (bf16[8,1024]{1,0:T(8,128)(2,1)S(1)}, bf16[8,1024]{1,0:T(8,128)(2,1)S(1)}, u32[]{:S(2)}, u32[]{:S(2)}) collective-permute-start(bf16[8,1024]{1,0:T(8,128)(2,1)S(1)} %cube.1.weights_ref), channel_id=1, source_target_pairs={{0,1},{1,0},{2,3},{3,2},{4,5},{5,4},{6,7},{7,6},{8,9},{9,8},{10,11... | collective-permute-start | bytes 49160 | tf_op jit(solution)/shard_map/ppermute | solution.py:217
  16.1 0.2 %prepare.1 = (bf16[2048,128]{1,0:T(8,128)(2,1)S(1)}, s32[2,8,128]{2,1,0:T(8,128)S(1)}, s32[2,8,128]{2,1,0:T(8,128)S(1)}, s32[2,8,128]{2,1,0:T(8,128)S(1)}, f32[2,8,512]{2,1,0:T(8,128)S(1)}) custom-call(bf16[128,2048]{1,0:T(8,128)(2,1)S(1)} %get-tuple-element.15.lagged_ref, bf16[16,512]{1,0:T(8,128)(2,1)S(1)} %bitcast.6, ...), custom_call_target="tpu_custom_call" | custom-call | flops 33554432 | bytes 2097152 | tf_op jit(solution)/shard_map/prepare/pallas_call | solution.py:278
  16.3 0.4 %adjoint_own.1 = (f32[8,512]{1,0:T(8,128)S(1)}, f32[1,1024]{1,0:T(1,128)S(1)}) custom-call(s32[1]{0:T(128)S(6)} %copy.7.mask_ref, bf16[8,1024]{1,0:T(8,128)(2,1)S(1)} %cube.1.weights_ref, bf16[2048,128]{1,0:T(8,128)(2,1)S(1)} %get-tuple-element.19.turned_ref, s32[2,8,128]{2,1,0:T(8,128)S(1)} %get-tuple-element.20.whole_ref, ...), custom_call_target="tpu_custom_call" | custom-call | flops 33554432 | bytes 2097152 | tf_op jit(solution)/shard_map/adjoint_own/pallas_call | solution.py:307
  16.7 0.3 %collective-permute-done.5.others_ref = bf16[8,1024]{1,0:T(8,128)(2,1)S(1)} collective-permute-done((bf16[8,1024]{1,0:T(8,128)(2,1)S(1)}, bf16[8,1024]{1,0:T(8,128)(2,1)S(1)}, u32[]{:S(2)}, u32[]{:S(2)}) %collective-permute-start.5) | collective-permute-done | bytes 16416 | tf_op jit(solution)/shard_map/ppermute | solution.py:217
  17.0 1.0 %adjoint_other.1 = (bf16[16,512]{1,0:T(8,128)(2,1)}, bf16[1,1024]{1,0:T(2,128)(2,1)}) custom-call(s32[1]{0:T(128)S(6)} %copy.7.mask_ref, bf16[8,1024]{1,0:T(8,128)(2,1)S(1)} %collective-permute-done.5.others_ref, f32[8,512]{1,0:T(8,128)S(1)} %get-tuple-element.24.ready_ref, f32[1,1024]{1,0:T(1,128)S(1)} %get-tuple-element.25.found_ref, ...), custom_call_target="tpu_custom_call" | custom-call | tf_op jit(solution)/shard_map/adjoint_other/pallas_call | solution.py:319
  (3 shorter events, 0.0 us)
Async XLA Ops:
  0.6 0.7 %copy-start = (bf16[16,1,512]{2,0,1:T(8,128)(2,1)S(1)}, bf16[16,1,512]{2,0,1:T(8,128)(2,1)}, u32[]{:S(2)}) copy-start(bf16[16,1,512]{2,0,1:T(8,128)(2,1)} %param.6) | copy-start | bytes 49156
  0.6 0.7 %copy-start.1 = (bf16[1,2048]{1,0:T(2,128)(2,1)S(1)}, bf16[1,2048]{1,0:T(2,128)(2,1)}, u32[]{:S(2)}) copy-start(bf16[1,2048]{1,0:T(2,128)(2,1)} %trace_ref.1) | copy-start | bytes 12292
  2.4 1.4 %collective-permute-start = (f32[8,1152]{1,0:T(8,128)S(1)}, f32[8,1152]{1,0:T(8,128)S(1)}, u32[]{:S(2)}, u32[]{:S(2)}) collective-permute-start(f32[8,1152]{1,0:T(8,128)S(1)} %get-tuple-element.17), channel_id=1, source_target_pairs={{0,1},{1,0},{2,3},{3,2},{4,5},{5,4},{6,7},{7,6},{8,9},{9,8},{10,11... | collective-permute-start | bytes 110600 | tf_op jit(solution)/shard_map/ppermute | solution.py:217
  3.8 5.8 %collective-permute-start.1 = (f32[8,1152]{1,0:T(8,128)S(1)}, f32[8,1152]{1,0:T(8,128)S(1)}, u32[]{:S(2)}, u32[]{:S(2)}) collective-permute-start(f32[8,1152]{1,0:T(8,128)S(1)} %add.12), channel_id=1, source_target_pairs={{0,6},{1,7},{2,4},{3,5},{4,2},{5,3},{6,0},{7,1},{8,14},{9,15},{10,... | collective-permute-start | bytes 110600 | tf_op jit(solution)/shard_map/ppermute | solution.py:217
  7.6 3.7 %collective-permute-start.2 = (f32[8,1152]{1,0:T(8,128)S(1)}, f32[8,1152]{1,0:T(8,128)S(1)}, u32[]{:S(2)}, u32[]{:S(2)}) collective-permute-start(f32[8,1152]{1,0:T(8,128)S(1)} %add.12), channel_id=1, source_target_pairs={{0,5},{1,4},{2,7},{3,6},{4,1},{5,0},{6,3},{7,2},{8,13},{9,12},{10,... | collective-permute-start | bytes 110600 | tf_op jit(solution)/shard_map/ppermute | solution.py:217
  7.7 3.7 %collective-permute-start.3 = (f32[8,1152]{1,0:T(8,128)S(1)}, f32[8,1152]{1,0:T(8,128)S(1)}, u32[]{:S(2)}, u32[]{:S(2)}) collective-permute-start(f32[8,1152]{1,0:T(8,128)S(1)} %add.12), channel_id=1, source_target_pairs={{0,3},{1,2},{2,1},{3,0},{4,7},{5,6},{6,5},{7,4},{8,11},{9,10},{10,... | collective-permute-start | bytes 110600 | tf_op jit(solution)/shard_map/ppermute | solution.py:217
  11.4 4.3 %collective-permute-start.4 = (f32[8,1152]{1,0:T(8,128)S(1)}, f32[8,1152]{1,0:T(8,128)S(1)}, u32[]{:S(2)}, u32[]{:S(2)}) collective-permute-start(f32[8,1152]{1,0:T(8,128)S(1)} %add_add_fusion.held_ref), channel_id=1, source_target_pairs={{0,9},{1,8},{2,11},{3,10},{4,13},{5,12},{6,15},{7,14},{8,1},{9,0},... | collective-permute-start | bytes 110600 | tf_op jit(solution)/shard_map/ppermute | solution.py:217
  15.8 1.2 %collective-permute-start.5 = (bf16[8,1024]{1,0:T(8,128)(2,1)S(1)}, bf16[8,1024]{1,0:T(8,128)(2,1)S(1)}, u32[]{:S(2)}, u32[]{:S(2)}) collective-permute-start(bf16[8,1024]{1,0:T(8,128)(2,1)S(1)} %cube.1.weights_ref), channel_id=1, source_target_pairs={{0,1},{1,0},{2,3},{3,2},{4,5},{5,4},{6,7},{7,6},{8,9},{9,8},{10,11... | collective-permute-start | bytes 49160 | tf_op jit(solution)/shard_map/ppermute | solution.py:217

commit v3 on v2

--- a/solution.py
+++ b/solution.py
@@ -36,14 +36,24 @@
     return [value[:, i : i + LANES] for i in range(0, value.shape[1], LANES)]
 
 
+def lag(blocks, step, lane):
+    turned = [pltpu.roll(block, LANES - step, 1) for block in blocks]
+    kept = lane < LANES - step
+    return [jnp.where(kept, t, n) for t, n in zip(turned, turned[1:] + turned[-1:])]
+
+
 def hankel(trace):
-    win = trace.shape[1]
-    base = jnp.broadcast_to(trace.astype(jnp.float32), (8, win))
-    row = lax.broadcasted_iota(jnp.int32, (8, win), 0)
+    shape = (8, LANES)
+    blocks = [jnp.broadcast_to(block, shape) for block in blocks_of(trace.astype(jnp.float32))]
+    row, lane = (lax.broadcasted_iota(jnp.int32, shape, axis) for axis in (0, 1))
     for step in (1, 2, 4):
-        base = jnp.where((row & step) != 0, pltpu.roll(base, win - step, 1), base)
-    rows = [base] + [pltpu.roll(base, win - step, 1) for step in range(8, LANES, 8)]
-    return jnp.concatenate(rows, axis=0).astype(jnp.bfloat16)
+        odd = (row & step) != 0
+        blocks = [jnp.where(odd, n, o) for n, o in zip(lag(blocks, step, lane), blocks)]
+    pairs = zip(blocks, lag(blocks, 8, lane))
+    blocks = [jnp.concatenate(pair, axis=0).astype(jnp.bfloat16) for pair in pairs]
+    lane = lax.broadcasted_iota(jnp.int32, (16, LANES), 1)
+    rows = [blocks] + [lag(blocks, step, lane) for step in range(16, LANES, 16)]
+    return [jnp.concatenate(column, axis=0) for column in list(zip(*rows))[:-1]]
 
 
 def shifts(moves_ref, which):
@@ -52,30 +62,21 @@
     return moves // LANES, moves % LANES
 
 
-def correlate(
-    span, which, mask_ref, lagged_ref, templates_ref, moves_ref, partial_ref, moves_ready=None
-):
-    length = templates_ref.shape[1]
+def correlate(span, which, mask_ref, tiles, templates_ref, moves_ref, partial_ref, moves_ready):
     widened = half_of(templates_ref[...].astype(jnp.float32), which)
     count = widened.shape[0]
     normed = widened * lax.rsqrt(jnp.sum(widened * widened, axis=1, keepdims=True) + 1e-06)
     pieces = blocks_of(normed)
+    stacked = jnp.concatenate(pieces, axis=0).astype(jnp.bfloat16)
     lags = span + MOVE
-    products = jnp.dot(
-        jnp.concatenate(pieces, axis=0).astype(jnp.bfloat16),
-        lagged_ref[:, : lags + length - LANES],
-        preferred_element_type=jnp.float32,
-    )
+    products = [jnp.dot(stacked, tile, preferred_element_type=jnp.float32) for tile in tiles]
+    products = [block for product in products for block in blocks_of(product)]
+    moves_ready()
+    whole, rest = shifts(moves_ref, which)
     found = []
-    for lag in range(0, lags, LANES):
-        terms = [
-            products[i * count : (i + 1) * count, lag + i * LANES : lag + (i + 1) * LANES]
-            for i in range(len(pieces))
-        ]
+    for j in range(lags // LANES):
+        terms = [products[j + i][i * count : (i + 1) * count] for i in range(len(pieces))]
         found.append(functools.reduce(jnp.add, terms))
-    if moves_ready is not None:
-        moves_ready()
-    whole, rest = shifts(moves_ref, which)
     lane = lax.broadcasted_iota(jnp.int32, (count, LANES), 1)
     source = (lane + rest) % LANES
     inside = lane + rest < LANES
@@ -111,17 +112,21 @@
         moves_copy.start()
         slots_copy.start()
 
-    lagged_ref[...] = hankel(trace_ref[...])
+    blocks = hankel(trace_ref[...])
+    tiles = [jnp.concatenate(blocks[i : i + 2], axis=1) for i in range(0, len(blocks), 2)]
+    for i, tile in enumerate(tiles):
+        lagged_ref[:, i * 2 * LANES : i * 2 * LANES + tile.shape[1]] = tile
     other = 1 - side(stations)
     correlate(
-        span, other, mask_ref, lagged_ref, templates_ref, moves_ref, partial_ref, moves_copy.wait
+        span, other, mask_ref, tiles, templates_ref, moves_ref, partial_ref, moves_copy.wait
     )
     slots_copy.wait()
 
 
 def kept_kernel(span, stations, mask_ref, lagged_ref, templates_ref, moves_ref, partial_ref):
     own = side(stations)
-    correlate(span, own, mask_ref, lagged_ref, templates_ref, moves_ref, partial_ref)
+    tiles = [lagged_ref[...]]
+    correlate(span, own, mask_ref, tiles, templates_ref, moves_ref, partial_ref, lambda: None)
 
 
 def cube_kernel(span, held_ref, got_ref, weights_ref):
@@ -168,7 +173,7 @@
         value = [placed[j - i] if 0 <= j - i < len(placed) else zero for i in range(pieces)]
         spread[:, j * LANES : (j + 1) * LANES] = jnp.concatenate(value, axis=0).astype(jnp.bfloat16)
     products = jnp.dot(
-        spread[...], turned_ref[: spread.shape[1], :], preferred_element_type=jnp.float32
+        spread[...], turned_ref[...], preferred_element_type=jnp.float32
     )
     update = jnp.concatenate(
         [products[i * count : (i + 1) * count] for i in range(pieces)], axis=1
@@ -257,7 +262,7 @@
         functools.partial(sent_kernel, span, stations),
         out_shape=(
             pltpu.VMEM((half, span + LANES), jnp.float32),
-            pltpu.VMEM((LANES, win), jnp.bfloat16),
+            pltpu.VMEM((LANES, win - LANES), jnp.bfloat16),
             pltpu.VMEM((1, count), jnp.int32),
             pltpu.VMEM((1, count), jnp.int32),
         ),
@@ -278,7 +283,7 @@
     ahead = pl.pallas_call(
         functools.partial(prepare_kernel, stations, owned),
         out_shape=(
-            pltpu.VMEM((win, LANES), jnp.bfloat16),
+            pltpu.VMEM((win - LANES, LANES), jnp.bfloat16),
             pltpu.VMEM((2, half, LANES), jnp.int32),
             pltpu.VMEM((2, half, LANES), jnp.int32),
             pltpu.VMEM((2, half, LANES), jnp.int32),

time: 18.2 us -> 18.1 us (level)
  no operation moved by 1% of the time
where the time goes in v3:
time: 18.1 us; the launch traced here: 17.9 us
  starting transfers between devices  7.49 us (41%)
  waiting for transfers between devices  6.07 us (34%)
  Pallas kernels  2.9 us (16%)
  between operations  1.33 us (7%)
    ppermute x6, starting transfers between devices, exchange(): return lax.ppermute(rows, 'sta', [(i, i ^ step) for i in range(stations)])  7.49 us
    ppermute x6, waiting for transfers between devices, exchange(): return lax.ppermute(rows, 'sta', [(i, i ^ step) for i in range(stations)])  6.07 us
    pallas_call x1, Pallas kernels, whole_step(): pl.pallas_call(functools.partial(other_kernel, stations, owned), out_shap...  0.97 us
    pallas_call x1, Pallas kernels, whole_step(): pl.pallas_call(functools.partial(sent_kernel, span, stations), out_shape=...  0.91 us
  transfers between devices with their start and end apart: 6, of which 5 were waited for; matrix products, arithmetic and copies ran while one was open for 0% of the time, Pallas kernels for 5%

profile of v3, /device:TPU:0, one launch (start us, length us, event | category | flops | bytes accessed | tf_op | source)
XLA Modules:
  0.0 17.9 jit_solution(3145717584955761220)
XLA Ops:
  0.6 0.0 copy-start
  0.6 0.0 copy-start.1
  1.3 0.0 copy-done
  1.3 0.0 copy-done.1
  1.4 0.9 %correlate_sent.1 = (f32[8,1152]{1,0:T(8,128)S(1)}, bf16[128,1920]{1,0:T(8,128)(2,1)S(1)}, s32[1,16]{1,0:T(1,128)S(1)}, s32[1,16]{1,0:T(1,128)S(1)}) custom-call(s32[1]{0:T(128)S(6)} %copy.7.mask_ref, f32[8,128]{1,0:T(8,128)S(1)} %lead.1.lead_ref, bf16[1,2048]{1,0:T(2,128)(2,1)S(1)} %copy-done.1, bf16[16,512]{1,0:T(8,128)(2,1)S(1)} %bitcast.4, ...), custom_call_target="tpu_custom_call" | custom-call | tf_op jit(solution)/shard_map/correlate_sent/pallas_call | solution.py:261
  2.3 0.6 %collective-permute-start = (f32[8,1152]{1,0:T(8,128)S(1)}, f32[8,1152]{1,0:T(8,128)S(1)}, u32[]{:S(2)}, u32[]{:S(2)}) collective-permute-start(f32[8,1152]{1,0:T(8,128)S(1)} %get-tuple-element.17), channel_id=1, source_target_pairs={{0,1},{1,0},{2,3},{3,2},{4,5},{5,4},{6,7},{7,6},{8,9},{9,8},{10,11... | collective-permute-start | bytes 110600 | tf_op jit(solution)/shard_map/ppermute | solution.py:222
  2.8 0.3 %correlate_kept.1 = f32[8,1152]{1,0:T(8,128)S(1)} custom-call(s32[1]{0:T(128)S(6)} %copy.7.mask_ref, bf16[128,1920]{1,0:T(8,128)(2,1)S(1)} %get-tuple-element.15.lagged_ref, bf16[16,512]{1,0:T(8,128)(2,1)S(1)} %bitcast.5, s32[1,16]{1,0:T(1,128)S(1)} %get-tuple-element.16.moves_ref), custom_call_target="tpu_custom_call" | custom-call | flops 33554432 | bytes 2097152 | tf_op jit(solution)/shard_map/correlate_kept/pallas_call | solution.py:275
  3.2 0.5 %collective-permute-done = f32[8,1152]{1,0:T(8,128)S(1)} collective-permute-done((f32[8,1152]{1,0:T(8,128)S(1)}, f32[8,1152]{1,0:T(8,128)S(1)}, u32[]{:S(2)}, u32[]{:S(2)}) %collective-permute-start) | collective-permute-done | bytes 36896 | tf_op jit(solution)/shard_map/ppermute | solution.py:222
  3.7 3.8 %collective-permute-start.1 = (f32[8,1152]{1,0:T(8,128)S(1)}, f32[8,1152]{1,0:T(8,128)S(1)}, u32[]{:S(2)}, u32[]{:S(2)}) collective-permute-start(f32[8,1152]{1,0:T(8,128)S(1)} %add.12), channel_id=1, source_target_pairs={{0,6},{1,7},{2,4},{3,5},{4,2},{5,3},{6,0},{7,1},{8,14},{9,15},{10,... | collective-permute-start | bytes 110600 | tf_op jit(solution)/shard_map/ppermute | solution.py:222
  7.5 0.0 collective-permute-start.2
  7.5 0.4 %collective-permute-start.3 = (f32[8,1152]{1,0:T(8,128)S(1)}, f32[8,1152]{1,0:T(8,128)S(1)}, u32[]{:S(2)}, u32[]{:S(2)}) collective-permute-start(f32[8,1152]{1,0:T(8,128)S(1)} %add.12), channel_id=1, source_target_pairs={{0,3},{1,2},{2,1},{3,0},{4,7},{5,6},{6,5},{7,4},{8,11},{9,10},{10,... | collective-permute-start | bytes 110600 | tf_op jit(solution)/shard_map/ppermute | solution.py:222
  7.9 1.6 %collective-permute-done.1 = f32[8,1152]{1,0:T(8,128)S(1)} collective-permute-done((f32[8,1152]{1,0:T(8,128)S(1)}, f32[8,1152]{1,0:T(8,128)S(1)}, u32[]{:S(2)}, u32[]{:S(2)}) %collective-permute-start.1) | collective-permute-done | bytes 36896 | tf_op jit(solution)/shard_map/ppermute | solution.py:222
  9.5 1.8 %collective-permute-done.2 = f32[8,1152]{1,0:T(8,128)S(1)} collective-permute-done((f32[8,1152]{1,0:T(8,128)S(1)}, f32[8,1152]{1,0:T(8,128)S(1)}, u32[]{:S(2)}, u32[]{:S(2)}) %collective-permute-start.2) | collective-permute-done | bytes 36896 | tf_op jit(solution)/shard_map/ppermute | solution.py:222
  11.2 0.0 collective-permute-done.3
  11.3 2.5 %collective-permute-start.4 = (f32[8,1152]{1,0:T(8,128)S(1)}, f32[8,1152]{1,0:T(8,128)S(1)}, u32[]{:S(2)}, u32[]{:S(2)}) collective-permute-start(f32[8,1152]{1,0:T(8,128)S(1)} %add_add_fusion.held_ref), channel_id=1, source_target_pairs={{0,9},{1,8},{2,11},{3,10},{4,13},{5,12},{6,15},{7,14},{8,1},{9,0},... | collective-permute-start | bytes 110600 | tf_op jit(solution)/shard_map/ppermute | solution.py:222
  13.8 1.9 %collective-permute-done.4.got_ref = f32[8,1152]{1,0:T(8,128)S(1)} collective-permute-done((f32[8,1152]{1,0:T(8,128)S(1)}, f32[8,1152]{1,0:T(8,128)S(1)}, u32[]{:S(2)}, u32[]{:S(2)}) %collective-permute-start.4) | collective-permute-done | bytes 36896 | tf_op jit(solution)/shard_map/ppermute | solution.py:222
  15.6 0.1 cube.1.weights_ref
  15.7 0.2 %collective-permute-start.5 = (bf16[8,1024]{1,0:T(8,128)(2,1)S(1)}, bf16[8,1024]{1,0:T(8,128)(2,1)S(1)}, u32[]{:S(2)}, u32[]{:S(2)}) collective-permute-start(bf16[8,1024]{1,0:T(8,128)(2,1)S(1)} %cube.1.weights_ref), channel_id=1, source_target_pairs={{0,1},{1,0},{2,3},{3,2},{4,5},{5,4},{6,7},{7,6},{8,9},{9,8},{10,11... | collective-permute-start | bytes 49160 | tf_op jit(solution)/shard_map/ppermute | solution.py:222
  15.9 0.2 %prepare.1 = (bf16[1920,128]{1,0:T(8,128)(2,1)S(1)}, s32[2,8,128]{2,1,0:T(8,128)S(1)}, s32[2,8,128]{2,1,0:T(8,128)S(1)}, s32[2,8,128]{2,1,0:T(8,128)S(1)}, f32[2,8,512]{2,1,0:T(8,128)S(1)}) custom-call(bf16[128,1920]{1,0:T(8,128)(2,1)S(1)} %get-tuple-element.15.lagged_ref, bf16[16,512]{1,0:T(8,128)(2,1)S(1)} %bitcast.6, ...), custom_call_target="tpu_custom_call" | custom-call | flops 33554432 | bytes 2097152 | tf_op jit(solution)/shard_map/prepare/pallas_call | solution.py:283
  16.2 0.4 %adjoint_own.1 = (f32[8,512]{1,0:T(8,128)S(1)}, f32[1,1024]{1,0:T(1,128)S(1)}) custom-call(s32[1]{0:T(128)S(6)} %copy.7.mask_ref, bf16[8,1024]{1,0:T(8,128)(2,1)S(1)} %cube.1.weights_ref, bf16[1920,128]{1,0:T(8,128)(2,1)S(1)} %get-tuple-element.19.turned_ref, s32[2,8,128]{2,1,0:T(8,128)S(1)} %get-tuple-element.20.whole_ref, ...), custom_call_target="tpu_custom_call" | custom-call | flops 33554432 | bytes 2097152 | tf_op jit(solution)/shard_map/adjoint_own/pallas_call | solution.py:312
  16.5 0.3 %collective-permute-done.5.others_ref = bf16[8,1024]{1,0:T(8,128)(2,1)S(1)} collective-permute-done((bf16[8,1024]{1,0:T(8,128)(2,1)S(1)}, bf16[8,1024]{1,0:T(8,128)(2,1)S(1)}, u32[]{:S(2)}, u32[]{:S(2)}) %collective-permute-start.5) | collective-permute-done | bytes 16416 | tf_op jit(solution)/shard_map/ppermute | solution.py:222
  16.9 1.0 %adjoint_other.1 = (bf16[16,512]{1,0:T(8,128)(2,1)}, bf16[1,1024]{1,0:T(2,128)(2,1)}) custom-call(s32[1]{0:T(128)S(6)} %copy.7.mask_ref, bf16[8,1024]{1,0:T(8,128)(2,1)S(1)} %collective-permute-done.5.others_ref, f32[8,512]{1,0:T(8,128)S(1)} %get-tuple-element.24.ready_ref, f32[1,1024]{1,0:T(1,128)S(1)} %get-tuple-element.25.found_ref, ...), custom_call_target="tpu_custom_call" | custom-call | tf_op jit(solution)/shard_map/adjoint_other/pallas_call | solution.py:324
  (3 shorter events, 0.0 us)
Async XLA Ops:
  0.6 0.7 %copy-start = (bf16[16,1,512]{2,0,1:T(8,128)(2,1)S(1)}, bf16[16,1,512]{2,0,1:T(8,128)(2,1)}, u32[]{:S(2)}) copy-start(bf16[16,1,512]{2,0,1:T(8,128)(2,1)} %param.6) | copy-start | bytes 49156
  0.6 0.7 %copy-start.1 = (bf16[1,2048]{1,0:T(2,128)(2,1)S(1)}, bf16[1,2048]{1,0:T(2,128)(2,1)}, u32[]{:S(2)}) copy-start(bf16[1,2048]{1,0:T(2,128)(2,1)} %trace_ref.1) | copy-start | bytes 12292
  2.3 1.4 %collective-permute-start = (f32[8,1152]{1,0:T(8,128)S(1)}, f32[8,1152]{1,0:T(8,128)S(1)}, u32[]{:S(2)}, u32[]{:S(2)}) collective-permute-start(f32[8,1152]{1,0:T(8,128)S(1)} %get-tuple-element.17), channel_id=1, source_target_pairs={{0,1},{1,0},{2,3},{3,2},{4,5},{5,4},{6,7},{7,6},{8,9},{9,8},{10,11... | collective-permute-start | bytes 110600 | tf_op jit(solution)/shard_map/ppermute | solution.py:222
  3.7 5.8 %collective-permute-start.1 = (f32[8,1152]{1,0:T(8,128)S(1)}, f32[8,1152]{1,0:T(8,128)S(1)}, u32[]{:S(2)}, u32[]{:S(2)}) collective-permute-start(f32[8,1152]{1,0:T(8,128)S(1)} %add.12), channel_id=1, source_target_pairs={{0,6},{1,7},{2,4},{3,5},{4,2},{5,3},{6,0},{7,1},{8,14},{9,15},{10,... | collective-permute-start | bytes 110600 | tf_op jit(solution)/shard_map/ppermute | solution.py:222
  7.5 3.7 %collective-permute-start.2 = (f32[8,1152]{1,0:T(8,128)S(1)}, f32[8,1152]{1,0:T(8,128)S(1)}, u32[]{:S(2)}, u32[]{:S(2)}) collective-permute-start(f32[8,1152]{1,0:T(8,128)S(1)} %add.12), channel_id=1, source_target_pairs={{0,5},{1,4},{2,7},{3,6},{4,1},{5,0},{6,3},{7,2},{8,13},{9,12},{10,... | collective-permute-start | bytes 110600 | tf_op jit(solution)/shard_map/ppermute | solution.py:222
  7.5 3.7 %collective-permute-start.3 = (f32[8,1152]{1,0:T(8,128)S(1)}, f32[8,1152]{1,0:T(8,128)S(1)}, u32[]{:S(2)}, u32[]{:S(2)}) collective-permute-start(f32[8,1152]{1,0:T(8,128)S(1)} %add.12), channel_id=1, source_target_pairs={{0,3},{1,2},{2,1},{3,0},{4,7},{5,6},{6,5},{7,4},{8,11},{9,10},{10,... | collective-permute-start | bytes 110600 | tf_op jit(solution)/shard_map/ppermute | solution.py:222
  11.3 4.3 %collective-permute-start.4 = (f32[8,1152]{1,0:T(8,128)S(1)}, f32[8,1152]{1,0:T(8,128)S(1)}, u32[]{:S(2)}, u32[]{:S(2)}) collective-permute-start(f32[8,1152]{1,0:T(8,128)S(1)} %add_add_fusion.held_ref), channel_id=1, source_target_pairs={{0,9},{1,8},{2,11},{3,10},{4,13},{5,12},{6,15},{7,14},{8,1},{9,0},... | collective-permute-start | bytes 110600 | tf_op jit(solution)/shard_map/ppermute | solution.py:222
  15.7 1.2 %collective-permute-start.5 = (bf16[8,1024]{1,0:T(8,128)(2,1)S(1)}, bf16[8,1024]{1,0:T(8,128)(2,1)S(1)}, u32[]{:S(2)}, u32[]{:S(2)}) collective-permute-start(bf16[8,1024]{1,0:T(8,128)(2,1)S(1)} %cube.1.weights_ref), channel_id=1, source_target_pairs={{0,1},{1,0},{2,3},{3,2},{4,5},{5,4},{6,7},{7,6},{8,9},{9,8},{10,11... | collective-permute-start | bytes 49160 | tf_op jit(solution)/shard_map/ppermute | solution.py:222

commit v4 on v3

--- a/solution.py
+++ b/solution.py
@@ -217,18 +217,21 @@
     updated_ref[...] = jnp.concatenate([low, high], axis=0).astype(jnp.bfloat16)
 
 
-def exchange(rows, step):
+def exchange(rows, steps):
     stations = lax.axis_size("sta")
-    return lax.ppermute(rows, "sta", [(i, i ^ step) for i in range(stations)])
+    pairs = [(i, i ^ steps[i.bit_count() % 2]) for i in range(stations)]
+    return lax.ppermute(rows, "sta", pairs)
 
 
 def stages(stations):
     bits = [1 << i for i in range(1, stations.bit_length() - 1)]
-    pairs = [bits[i : i + 2] for i in range(0, len(bits), 2)]
-    return [
-        [pair[0] | pair[1], pair[1] | 1, pair[0] | 1] if len(pair) == 2 else [pair[0] | 1]
-        for pair in pairs
-    ]
+    found = []
+    for low, high in zip(bits[::2], bits[1::2]):
+        low, high, both = low | 1, high | 1, low | high
+        found.append([(both, low), (high, both), (low, high)])
+    if len(bits) % 2:
+        found.append([(bits[-1] | 1, bits[-1] | 1)])
+    return found
 
 
 def whole_step(traces, templates, moveouts, channel_mask, owner_slot):
@@ -295,12 +298,12 @@
         name="prepare",
     )(near(lagged), own_templates, moves, slots)
     ahead = [near(value) for value in ahead]
-    held, got = kept, exchange(sent, 1)
+    held, got = kept, exchange(sent, (1, 1))
     for hops in stages(stations):
         held = held + got
         parts = []
-        for step in hops:
-            parts.append(exchange(held, step))
+        for steps in hops:
+            parts.append(exchange(held, steps))
         got = functools.reduce(jnp.add, parts)
     weights = pl.pallas_call(
         functools.partial(cube_kernel, span),
@@ -331,7 +334,7 @@
         out_specs=(vector, vector),
         scratch_shapes=spread,
         name="adjoint_other",
-    )(channel_mask, near(exchange(weights, 1)), near(ready), near(found), *ahead)
+    )(channel_mask, near(exchange(weights, (1, 1))), near(ready), near(found), *ahead)
     return (updated.reshape(count, 1, length), own)
 
 

time: 18.1 us -> 18 us (level)
  waiting for transfers between devices: 6.07 us -> 5.42 us
  starting transfers between devices: 7.49 us -> 7.98 us
    ppermute x6, waiting for transfers between devices: 6.07 us -> 5.42 us  [exchange(): return lax.ppermute(rows, 'sta', pairs)]
    ppermute x6, starting transfers between devices: 7.49 us -> 7.98 us  [exchange(): return lax.ppermute(rows, 'sta', pairs)]
where the time goes in v4:
time: 18 us; the launch traced here: 17.7 us
  starting transfers between devices  7.98 us (44%)
  waiting for transfers between devices  5.42 us (30%)
  Pallas kernels  2.9 us (16%)
  between operations  1.33 us (7%)
    ppermute x6, starting transfers between devices, exchange(): return lax.ppermute(rows, 'sta', pairs)  7.98 us
    ppermute x6, waiting for transfers between devices, exchange(): return lax.ppermute(rows, 'sta', pairs)  5.42 us
    pallas_call x1, Pallas kernels, whole_step(): pl.pallas_call(functools.partial(other_kernel, stations, owned), out_shap...  0.97 us
    pallas_call x1, Pallas kernels, whole_step(): pl.pallas_call(functools.partial(sent_kernel, span, stations), out_shape=...  0.91 us
  transfers between devices with their start and end apart: 6, of which 5 were waited for; matrix products, arithmetic and copies ran while one was open for 0% of the time, Pallas kernels for 5%

profile of v4, /device:TPU:0, one launch (start us, length us, event | category | flops | bytes accessed | tf_op | source)
XLA Modules:
  0.0 17.7 jit_solution(17471439650705014541)
XLA Ops:
  0.6 0.0 copy-start
  0.6 0.0 copy-start.1
  1.3 0.0 copy-done
  1.3 0.0 copy-done.1
  1.4 0.9 %correlate_sent.1 = (f32[8,1152]{1,0:T(8,128)S(1)}, bf16[128,1920]{1,0:T(8,128)(2,1)S(1)}, s32[1,16]{1,0:T(1,128)S(1)}, s32[1,16]{1,0:T(1,128)S(1)}) custom-call(s32[1]{0:T(128)S(6)} %copy.7.mask_ref, f32[8,128]{1,0:T(8,128)S(1)} %lead.1.lead_ref, bf16[1,2048]{1,0:T(2,128)(2,1)S(1)} %copy-done.1, bf16[16,512]{1,0:T(8,128)(2,1)S(1)} %bitcast.4, ...), custom_call_target="tpu_custom_call" | custom-call | tf_op jit(solution)/shard_map/correlate_sent/pallas_call | solution.py:264
  2.3 0.6 %collective-permute-start = (f32[8,1152]{1,0:T(8,128)S(1)}, f32[8,1152]{1,0:T(8,128)S(1)}, u32[]{:S(2)}, u32[]{:S(2)}) collective-permute-start(f32[8,1152]{1,0:T(8,128)S(1)} %get-tuple-element.17), channel_id=1, source_target_pairs={{0,1},{1,0},{2,3},{3,2},{4,5},{5,4},{6,7},{7,6},{8,9},{9,8},{10,11... | collective-permute-start | bytes 110600 | tf_op jit(solution)/shard_map/ppermute | solution.py:223
  2.8 0.3 %correlate_kept.1 = f32[8,1152]{1,0:T(8,128)S(1)} custom-call(s32[1]{0:T(128)S(6)} %copy.7.mask_ref, bf16[128,1920]{1,0:T(8,128)(2,1)S(1)} %get-tuple-element.15.lagged_ref, bf16[16,512]{1,0:T(8,128)(2,1)S(1)} %bitcast.5, s32[1,16]{1,0:T(1,128)S(1)} %get-tuple-element.16.moves_ref), custom_call_target="tpu_custom_call" | custom-call | flops 33554432 | bytes 2097152 | tf_op jit(solution)/shard_map/correlate_kept/pallas_call | solution.py:278
  3.2 0.5 %collective-permute-done = f32[8,1152]{1,0:T(8,128)S(1)} collective-permute-done((f32[8,1152]{1,0:T(8,128)S(1)}, f32[8,1152]{1,0:T(8,128)S(1)}, u32[]{:S(2)}, u32[]{:S(2)}) %collective-permute-start) | collective-permute-done | bytes 36896 | tf_op jit(solution)/shard_map/ppermute | solution.py:223
  3.7 3.8 %collective-permute-start.1 = (f32[8,1152]{1,0:T(8,128)S(1)}, f32[8,1152]{1,0:T(8,128)S(1)}, u32[]{:S(2)}, u32[]{:S(2)}) collective-permute-start(f32[8,1152]{1,0:T(8,128)S(1)} %add.12), channel_id=1, source_target_pairs={{0,6},{1,2},{2,1},{3,5},{4,7},{5,3},{6,0},{7,4},{8,11},{9,15},{10,... | collective-permute-start | bytes 110600 | tf_op jit(solution)/shard_map/ppermute | solution.py:223
  7.5 0.0 collective-permute-start.2
  7.5 0.4 %collective-permute-start.3 = (f32[8,1152]{1,0:T(8,128)S(1)}, f32[8,1152]{1,0:T(8,128)S(1)}, u32[]{:S(2)}, u32[]{:S(2)}) collective-permute-start(f32[8,1152]{1,0:T(8,128)S(1)} %add.12), channel_id=1, source_target_pairs={{0,3},{1,4},{2,7},{3,0},{4,1},{5,6},{6,5},{7,2},{8,13},{9,10},{10,... | collective-permute-start | bytes 110600 | tf_op jit(solution)/shard_map/ppermute | solution.py:223
  7.9 1.6 %collective-permute-done.1 = f32[8,1152]{1,0:T(8,128)S(1)} collective-permute-done((f32[8,1152]{1,0:T(8,128)S(1)}, f32[8,1152]{1,0:T(8,128)S(1)}, u32[]{:S(2)}, u32[]{:S(2)}) %collective-permute-start.1) | collective-permute-done | bytes 36896 | tf_op jit(solution)/shard_map/ppermute | solution.py:223
  9.5 1.4 %collective-permute-done.2 = f32[8,1152]{1,0:T(8,128)S(1)} collective-permute-done((f32[8,1152]{1,0:T(8,128)S(1)}, f32[8,1152]{1,0:T(8,128)S(1)}, u32[]{:S(2)}, u32[]{:S(2)}) %collective-permute-start.2) | collective-permute-done | bytes 36896 | tf_op jit(solution)/shard_map/ppermute | solution.py:223
  10.9 0.0 collective-permute-done.3
  10.9 2.8 %collective-permute-start.4 = (f32[8,1152]{1,0:T(8,128)S(1)}, f32[8,1152]{1,0:T(8,128)S(1)}, u32[]{:S(2)}, u32[]{:S(2)}) collective-permute-start(f32[8,1152]{1,0:T(8,128)S(1)} %add_add_fusion.held_ref), channel_id=1, source_target_pairs={{0,9},{1,8},{2,11},{3,10},{4,13},{5,12},{6,15},{7,14},{8,1},{9,0},... | collective-permute-start | bytes 110600 | tf_op jit(solution)/shard_map/ppermute | solution.py:223
  13.8 1.6 %collective-permute-done.4.got_ref = f32[8,1152]{1,0:T(8,128)S(1)} collective-permute-done((f32[8,1152]{1,0:T(8,128)S(1)}, f32[8,1152]{1,0:T(8,128)S(1)}, u32[]{:S(2)}, u32[]{:S(2)}) %collective-permute-start.4) | collective-permute-done | bytes 36896 | tf_op jit(solution)/shard_map/ppermute | solution.py:223
  15.4 0.1 cube.1.weights_ref
  15.5 0.4 %collective-permute-start.5 = (bf16[8,1024]{1,0:T(8,128)(2,1)S(1)}, bf16[8,1024]{1,0:T(8,128)(2,1)S(1)}, u32[]{:S(2)}, u32[]{:S(2)}) collective-permute-start(bf16[8,1024]{1,0:T(8,128)(2,1)S(1)} %cube.1.weights_ref), channel_id=1, source_target_pairs={{0,1},{1,0},{2,3},{3,2},{4,5},{5,4},{6,7},{7,6},{8,9},{9,8},{10,11... | collective-permute-start | bytes 49160 | tf_op jit(solution)/shard_map/ppermute | solution.py:223
  15.9 0.2 %prepare.1 = (bf16[1920,128]{1,0:T(8,128)(2,1)S(1)}, s32[2,8,128]{2,1,0:T(8,128)S(1)}, s32[2,8,128]{2,1,0:T(8,128)S(1)}, s32[2,8,128]{2,1,0:T(8,128)S(1)}, f32[2,8,512]{2,1,0:T(8,128)S(1)}) custom-call(bf16[128,1920]{1,0:T(8,128)(2,1)S(1)} %get-tuple-element.15.lagged_ref, bf16[16,512]{1,0:T(8,128)(2,1)S(1)} %bitcast.6, ...), custom_call_target="tpu_custom_call" | custom-call | flops 33554432 | bytes 2097152 | tf_op jit(solution)/shard_map/prepare/pallas_call | solution.py:286
  16.1 0.4 %adjoint_own.1 = (f32[8,512]{1,0:T(8,128)S(1)}, f32[1,1024]{1,0:T(1,128)S(1)}) custom-call(s32[1]{0:T(128)S(6)} %copy.7.mask_ref, bf16[8,1024]{1,0:T(8,128)(2,1)S(1)} %cube.1.weights_ref, bf16[1920,128]{1,0:T(8,128)(2,1)S(1)} %get-tuple-element.19.turned_ref, s32[2,8,128]{2,1,0:T(8,128)S(1)} %get-tuple-element.20.whole_ref, ...), custom_call_target="tpu_custom_call" | custom-call | flops 33554432 | bytes 2097152 | tf_op jit(solution)/shard_map/adjoint_own/pallas_call | solution.py:315
  16.5 0.2 %collective-permute-done.5.others_ref = bf16[8,1024]{1,0:T(8,128)(2,1)S(1)} collective-permute-done((bf16[8,1024]{1,0:T(8,128)(2,1)S(1)}, bf16[8,1024]{1,0:T(8,128)(2,1)S(1)}, u32[]{:S(2)}, u32[]{:S(2)}) %collective-permute-start.5) | collective-permute-done | bytes 16416 | tf_op jit(solution)/shard_map/ppermute | solution.py:223
  16.7 1.0 %adjoint_other.1 = (bf16[16,512]{1,0:T(8,128)(2,1)}, bf16[1,1024]{1,0:T(2,128)(2,1)}) custom-call(s32[1]{0:T(128)S(6)} %copy.7.mask_ref, bf16[8,1024]{1,0:T(8,128)(2,1)S(1)} %collective-permute-done.5.others_ref, f32[8,512]{1,0:T(8,128)S(1)} %get-tuple-element.24.ready_ref, f32[1,1024]{1,0:T(1,128)S(1)} %get-tuple-element.25.found_ref, ...), custom_call_target="tpu_custom_call" | custom-call | tf_op jit(solution)/shard_map/adjoint_other/pallas_call | solution.py:327
  (3 shorter events, 0.0 us)
Async XLA Ops:
  0.6 0.7 %copy-start = (bf16[16,1,512]{2,0,1:T(8,128)(2,1)S(1)}, bf16[16,1,512]{2,0,1:T(8,128)(2,1)}, u32[]{:S(2)}) copy-start(bf16[16,1,512]{2,0,1:T(8,128)(2,1)} %param.6) | copy-start | bytes 49156
  0.6 0.7 %copy-start.1 = (bf16[1,2048]{1,0:T(2,128)(2,1)S(1)}, bf16[1,2048]{1,0:T(2,128)(2,1)}, u32[]{:S(2)}) copy-start(bf16[1,2048]{1,0:T(2,128)(2,1)} %trace_ref.1) | copy-start | bytes 12292
  2.3 1.4 %collective-permute-start = (f32[8,1152]{1,0:T(8,128)S(1)}, f32[8,1152]{1,0:T(8,128)S(1)}, u32[]{:S(2)}, u32[]{:S(2)}) collective-permute-start(f32[8,1152]{1,0:T(8,128)S(1)} %get-tuple-element.17), channel_id=1, source_target_pairs={{0,1},{1,0},{2,3},{3,2},{4,5},{5,4},{6,7},{7,6},{8,9},{9,8},{10,11... | collective-permute-start | bytes 110600 | tf_op jit(solution)/shard_map/ppermute | solution.py:223
  3.7 5.8 %collective-permute-start.1 = (f32[8,1152]{1,0:T(8,128)S(1)}, f32[8,1152]{1,0:T(8,128)S(1)}, u32[]{:S(2)}, u32[]{:S(2)}) collective-permute-start(f32[8,1152]{1,0:T(8,128)S(1)} %add.12), channel_id=1, source_target_pairs={{0,6},{1,2},{2,1},{3,5},{4,7},{5,3},{6,0},{7,4},{8,11},{9,15},{10,... | collective-permute-start | bytes 110600 | tf_op jit(solution)/shard_map/ppermute | solution.py:223
  7.5 3.4 %collective-permute-start.2 = (f32[8,1152]{1,0:T(8,128)S(1)}, f32[8,1152]{1,0:T(8,128)S(1)}, u32[]{:S(2)}, u32[]{:S(2)}) collective-permute-start(f32[8,1152]{1,0:T(8,128)S(1)} %add.12), channel_id=1, source_target_pairs={{0,5},{1,7},{2,4},{3,6},{4,2},{5,0},{6,3},{7,1},{8,14},{9,12},{10,... | collective-permute-start | bytes 110600 | tf_op jit(solution)/shard_map/ppermute | solution.py:223
  7.5 3.4 %collective-permute-start.3 = (f32[8,1152]{1,0:T(8,128)S(1)}, f32[8,1152]{1,0:T(8,128)S(1)}, u32[]{:S(2)}, u32[]{:S(2)}) collective-permute-start(f32[8,1152]{1,0:T(8,128)S(1)} %add.12), channel_id=1, source_target_pairs={{0,3},{1,4},{2,7},{3,0},{4,1},{5,6},{6,5},{7,2},{8,13},{9,10},{10,... | collective-permute-start | bytes 110600 | tf_op jit(solution)/shard_map/ppermute | solution.py:223
  10.9 4.5 %collective-permute-start.4 = (f32[8,1152]{1,0:T(8,128)S(1)}, f32[8,1152]{1,0:T(8,128)S(1)}, u32[]{:S(2)}, u32[]{:S(2)}) collective-permute-start(f32[8,1152]{1,0:T(8,128)S(1)} %add_add_fusion.held_ref), channel_id=1, source_target_pairs={{0,9},{1,8},{2,11},{3,10},{4,13},{5,12},{6,15},{7,14},{8,1},{9,0},... | collective-permute-start | bytes 110600 | tf_op jit(solution)/shard_map/ppermute | solution.py:223
  15.5 1.2 %collective-permute-start.5 = (bf16[8,1024]{1,0:T(8,128)(2,1)S(1)}, bf16[8,1024]{1,0:T(8,128)(2,1)S(1)}, u32[]{:S(2)}, u32[]{:S(2)}) collective-permute-start(bf16[8,1024]{1,0:T(8,128)(2,1)S(1)} %cube.1.weights_ref), channel_id=1, source_target_pairs={{0,1},{1,0},{2,3},{3,2},{4,5},{5,4},{6,7},{7,6},{8,9},{9,8},{10,11... | collective-permute-start | bytes 49160 | tf_op jit(solution)/shard_map/ppermute | solution.py:223

commit v5 on v4

--- a/solution.py
+++ b/solution.py
@@ -139,7 +139,9 @@
     stations, owned, lagged_ref, templates_ref, moves_ref, slots_ref, turned_ref, whole_ref,
     rest_ref, slots_out, initial_ref,
 ):
-    turned_ref[...] = lagged_ref[...].astype(jnp.float32).T.astype(jnp.bfloat16)
+    turned = lagged_ref[...].astype(jnp.float32).T.astype(jnp.bfloat16)
+    turned_ref[:, :LANES] = turned[:-LANES]
+    turned_ref[:, LANES:] = turned[LANES:]
     own = side(stations)
     templates = templates_ref[...].astype(jnp.float32)
     first = lax.axis_index("sta") * owned
@@ -168,13 +170,11 @@
             if 0 <= j - h < len(shifted):
                 value = jnp.where(whole == h, shifted[j - h], value)
         placed.append(value)
-    pieces = length // LANES
-    for j in range(len(placed) + pieces - 1):
-        value = [placed[j - i] if 0 <= j - i < len(placed) else zero for i in range(pieces)]
+    pieces = length // LANES // 2
+    for j in range(len(placed) + 2 * pieces - 2):
+        value = [placed[j - 2 * i] if 0 <= j - 2 * i < len(placed) else zero for i in range(pieces)]
         spread[:, j * LANES : (j + 1) * LANES] = jnp.concatenate(value, axis=0).astype(jnp.bfloat16)
-    products = jnp.dot(
-        spread[...], turned_ref[...], preferred_element_type=jnp.float32
-    )
+    products = jnp.dot(spread[...], turned_ref[...], preferred_element_type=jnp.float32)
     update = jnp.concatenate(
         [products[i * count : (i + 1) * count] for i in range(pieces)], axis=1
     )
@@ -247,7 +247,7 @@
     scalar = pl.BlockSpec(memory_space=pltpu.SMEM)
     vector = pl.BlockSpec(memory_space=pltpu.VMEM)
     near = functools.partial(pltpu.with_memory_space_constraint, memory_space=pltpu.VMEM)
-    spread = [pltpu.VMEM((half * length // LANES, win - LANES), jnp.bfloat16)]
+    spread = [pltpu.VMEM((half * length // LANES // 2, win - 2 * LANES), jnp.bfloat16)]
     work = pl.CostEstimate(
         flops=2 * count * length * win, bytes_accessed=LANES * win * 8, transcendentals=0
     )
@@ -286,7 +286,7 @@
     ahead = pl.pallas_call(
         functools.partial(prepare_kernel, stations, owned),
         out_shape=(
-            pltpu.VMEM((win - LANES, LANES), jnp.bfloat16),
+            pltpu.VMEM((win - 2 * LANES, 2 * LANES), jnp.bfloat16),
             pltpu.VMEM((2, half, LANES), jnp.int32),
             pltpu.VMEM((2, half, LANES), jnp.int32),
             pltpu.VMEM((2, half, LANES), jnp.int32),

time: 18 us -> 18 us (level)
  no operation moved by 1% of the time
where the time goes in v5:
time: 18 us; the launch traced here: 17.7 us
  starting transfers between devices  7.98 us (44%)
  waiting for transfers between devices  5.43 us (30%)
  Pallas kernels  2.93 us (16%)
  between operations  1.34 us (7%)
    ppermute x6, starting transfers between devices, exchange(): return lax.ppermute(rows, 'sta', pairs)  7.98 us
    ppermute x6, waiting for transfers between devices, exchange(): return lax.ppermute(rows, 'sta', pairs)  5.43 us
    pallas_call x1, Pallas kernels, whole_step(): pl.pallas_call(functools.partial(other_kernel, stations, owned), out_shap...  1.01 us
    pallas_call x1, Pallas kernels, whole_step(): pl.pallas_call(functools.partial(sent_kernel, span, stations), out_shape=...  0.91 us
  transfers between devices with their start and end apart: 6, of which 5 were waited for; matrix products, arithmetic and copies ran while one was open for 0% of the time, Pallas kernels for 5%

profile of v5, /device:TPU:0, one launch (start us, length us, event | category | flops | bytes accessed | tf_op | source)
XLA Modules:
  0.0 17.7 jit_solution(9630223513333309894)
XLA Ops:
  0.6 0.0 copy-start
  0.6 0.0 copy-start.1
  1.3 0.0 copy-done
  1.3 0.0 copy-done.1
  1.4 0.9 %correlate_sent.1 = (f32[8,1152]{1,0:T(8,128)S(1)}, bf16[128,1920]{1,0:T(8,128)(2,1)S(1)}, s32[1,16]{1,0:T(1,128)S(1)}, s32[1,16]{1,0:T(1,128)S(1)}) custom-call(s32[1]{0:T(128)S(6)} %copy.7.mask_ref, f32[8,128]{1,0:T(8,128)S(1)} %lead.1.lead_ref, bf16[1,2048]{1,0:T(2,128)(2,1)S(1)} %copy-done.1, bf16[16,512]{1,0:T(8,128)(2,1)S(1)} %bitcast.4, ...), custom_call_target="tpu_custom_call" | custom-call | tf_op jit(solution)/shard_map/correlate_sent/pallas_call | solution.py:264
  2.3 0.6 %collective-permute-start = (f32[8,1152]{1,0:T(8,128)S(1)}, f32[8,1152]{1,0:T(8,128)S(1)}, u32[]{:S(2)}, u32[]{:S(2)}) collective-permute-start(f32[8,1152]{1,0:T(8,128)S(1)} %get-tuple-element.17), channel_id=1, source_target_pairs={{0,1},{1,0},{2,3},{3,2},{4,5},{5,4},{6,7},{7,6},{8,9},{9,8},{10,11... | collective-permute-start | bytes 110600 | tf_op jit(solution)/shard_map/ppermute | solution.py:223
  2.8 0.4 %correlate_kept.1 = f32[8,1152]{1,0:T(8,128)S(1)} custom-call(s32[1]{0:T(128)S(6)} %copy.7.mask_ref, bf16[128,1920]{1,0:T(8,128)(2,1)S(1)} %get-tuple-element.15.lagged_ref, bf16[16,512]{1,0:T(8,128)(2,1)S(1)} %bitcast.5, s32[1,16]{1,0:T(1,128)S(1)} %get-tuple-element.16.moves_ref), custom_call_target="tpu_custom_call" | custom-call | flops 33554432 | bytes 2097152 | tf_op jit(solution)/shard_map/correlate_kept/pallas_call | solution.py:278
  3.2 0.5 %collective-permute-done = f32[8,1152]{1,0:T(8,128)S(1)} collective-permute-done((f32[8,1152]{1,0:T(8,128)S(1)}, f32[8,1152]{1,0:T(8,128)S(1)}, u32[]{:S(2)}, u32[]{:S(2)}) %collective-permute-start) | collective-permute-done | bytes 36896 | tf_op jit(solution)/shard_map/ppermute | solution.py:223
  3.7 3.8 %collective-permute-start.1 = (f32[8,1152]{1,0:T(8,128)S(1)}, f32[8,1152]{1,0:T(8,128)S(1)}, u32[]{:S(2)}, u32[]{:S(2)}) collective-permute-start(f32[8,1152]{1,0:T(8,128)S(1)} %add.12), channel_id=1, source_target_pairs={{0,6},{1,2},{2,1},{3,5},{4,7},{5,3},{6,0},{7,4},{8,11},{9,15},{10,... | collective-permute-start | bytes 110600 | tf_op jit(solution)/shard_map/ppermute | solution.py:223
  7.5 0.0 collective-permute-start.2
  7.5 0.4 %collective-permute-start.3 = (f32[8,1152]{1,0:T(8,128)S(1)}, f32[8,1152]{1,0:T(8,128)S(1)}, u32[]{:S(2)}, u32[]{:S(2)}) collective-permute-start(f32[8,1152]{1,0:T(8,128)S(1)} %add.12), channel_id=1, source_target_pairs={{0,3},{1,4},{2,7},{3,0},{4,1},{5,6},{6,5},{7,2},{8,13},{9,10},{10,... | collective-permute-start | bytes 110600 | tf_op jit(solution)/shard_map/ppermute | solution.py:223
  7.9 1.6 %collective-permute-done.1 = f32[8,1152]{1,0:T(8,128)S(1)} collective-permute-done((f32[8,1152]{1,0:T(8,128)S(1)}, f32[8,1152]{1,0:T(8,128)S(1)}, u32[]{:S(2)}, u32[]{:S(2)}) %collective-permute-start.1) | collective-permute-done | bytes 36896 | tf_op jit(solution)/shard_map/ppermute | solution.py:223
  9.5 1.4 %collective-permute-done.2 = f32[8,1152]{1,0:T(8,128)S(1)} collective-permute-done((f32[8,1152]{1,0:T(8,128)S(1)}, f32[8,1152]{1,0:T(8,128)S(1)}, u32[]{:S(2)}, u32[]{:S(2)}) %collective-permute-start.2) | collective-permute-done | bytes 36896 | tf_op jit(solution)/shard_map/ppermute | solution.py:223
  10.9 0.0 collective-permute-done.3
  10.9 2.8 %collective-permute-start.4 = (f32[8,1152]{1,0:T(8,128)S(1)}, f32[8,1152]{1,0:T(8,128)S(1)}, u32[]{:S(2)}, u32[]{:S(2)}) collective-permute-start(f32[8,1152]{1,0:T(8,128)S(1)} %add_add_fusion.held_ref), channel_id=1, source_target_pairs={{0,9},{1,8},{2,11},{3,10},{4,13},{5,12},{6,15},{7,14},{8,1},{9,0},... | collective-permute-start | bytes 110600 | tf_op jit(solution)/shard_map/ppermute | solution.py:223
  13.8 1.6 %collective-permute-done.4.got_ref = f32[8,1152]{1,0:T(8,128)S(1)} collective-permute-done((f32[8,1152]{1,0:T(8,128)S(1)}, f32[8,1152]{1,0:T(8,128)S(1)}, u32[]{:S(2)}, u32[]{:S(2)}) %collective-permute-start.4) | collective-permute-done | bytes 36896 | tf_op jit(solution)/shard_map/ppermute | solution.py:223
  15.4 0.1 cube.1.weights_ref
  15.5 0.4 %collective-permute-start.5 = (bf16[8,1024]{1,0:T(8,128)(2,1)S(1)}, bf16[8,1024]{1,0:T(8,128)(2,1)S(1)}, u32[]{:S(2)}, u32[]{:S(2)}) collective-permute-start(bf16[8,1024]{1,0:T(8,128)(2,1)S(1)} %cube.1.weights_ref), channel_id=1, source_target_pairs={{0,1},{1,0},{2,3},{3,2},{4,5},{5,4},{6,7},{7,6},{8,9},{9,8},{10,11... | collective-permute-start | bytes 49160 | tf_op jit(solution)/shard_map/ppermute | solution.py:223
  15.9 0.2 %prepare.1 = (bf16[1792,256]{1,0:T(8,128)(2,1)S(1)}, s32[2,8,128]{2,1,0:T(8,128)S(1)}, s32[2,8,128]{2,1,0:T(8,128)S(1)}, s32[2,8,128]{2,1,0:T(8,128)S(1)}, f32[2,8,512]{2,1,0:T(8,128)S(1)}) custom-call(bf16[128,1920]{1,0:T(8,128)(2,1)S(1)} %get-tuple-element.15.lagged_ref, bf16[16,512]{1,0:T(8,128)(2,1)S(1)} %bitcast.6, ...), custom_call_target="tpu_custom_call" | custom-call | flops 33554432 | bytes 2097152 | tf_op jit(solution)/shard_map/prepare/pallas_call | solution.py:286
  16.1 0.3 %adjoint_own.1 = (f32[8,512]{1,0:T(8,128)S(1)}, f32[1,1024]{1,0:T(1,128)S(1)}) custom-call(s32[1]{0:T(128)S(6)} %copy.7.mask_ref, bf16[8,1024]{1,0:T(8,128)(2,1)S(1)} %cube.1.weights_ref, bf16[1792,256]{1,0:T(8,128)(2,1)S(1)} %get-tuple-element.19.turned_ref, s32[2,8,128]{2,1,0:T(8,128)S(1)} %get-tuple-element.20.whole_ref, ...), custom_call_target="tpu_custom_call" | custom-call | flops 33554432 | bytes 2097152 | tf_op jit(solution)/shard_map/adjoint_own/pallas_call | solution.py:315
  16.5 0.3 %collective-permute-done.5.others_ref = bf16[8,1024]{1,0:T(8,128)(2,1)S(1)} collective-permute-done((bf16[8,1024]{1,0:T(8,128)(2,1)S(1)}, bf16[8,1024]{1,0:T(8,128)(2,1)S(1)}, u32[]{:S(2)}, u32[]{:S(2)}) %collective-permute-start.5) | collective-permute-done | bytes 16416 | tf_op jit(solution)/shard_map/ppermute | solution.py:223
  16.7 1.0 %adjoint_other.1 = (bf16[16,512]{1,0:T(8,128)(2,1)}, bf16[1,1024]{1,0:T(2,128)(2,1)}) custom-call(s32[1]{0:T(128)S(6)} %copy.7.mask_ref, bf16[8,1024]{1,0:T(8,128)(2,1)S(1)} %collective-permute-done.5.others_ref, f32[8,512]{1,0:T(8,128)S(1)} %get-tuple-element.24.ready_ref, f32[1,1024]{1,0:T(1,128)S(1)} %get-tuple-element.25.found_ref, ...), custom_call_target="tpu_custom_call" | custom-call | tf_op jit(solution)/shard_map/adjoint_other/pallas_call | solution.py:327
  (3 shorter events, 0.0 us)
Async XLA Ops:
  0.6 0.7 %copy-start = (bf16[16,1,512]{2,0,1:T(8,128)(2,1)S(1)}, bf16[16,1,512]{2,0,1:T(8,128)(2,1)}, u32[]{:S(2)}) copy-start(bf16[16,1,512]{2,0,1:T(8,128)(2,1)} %param.6) | copy-start | bytes 49156
  0.6 0.7 %copy-start.1 = (bf16[1,2048]{1,0:T(2,128)(2,1)S(1)}, bf16[1,2048]{1,0:T(2,128)(2,1)}, u32[]{:S(2)}) copy-start(bf16[1,2048]{1,0:T(2,128)(2,1)} %trace_ref.1) | copy-start | bytes 12292
  2.3 1.4 %collective-permute-start = (f32[8,1152]{1,0:T(8,128)S(1)}, f32[8,1152]{1,0:T(8,128)S(1)}, u32[]{:S(2)}, u32[]{:S(2)}) collective-permute-start(f32[8,1152]{1,0:T(8,128)S(1)} %get-tuple-element.17), channel_id=1, source_target_pairs={{0,1},{1,0},{2,3},{3,2},{4,5},{5,4},{6,7},{7,6},{8,9},{9,8},{10,11... | collective-permute-start | bytes 110600 | tf_op jit(solution)/shard_map/ppermute | solution.py:223
  3.7 5.8 %collective-permute-start.1 = (f32[8,1152]{1,0:T(8,128)S(1)}, f32[8,1152]{1,0:T(8,128)S(1)}, u32[]{:S(2)}, u32[]{:S(2)}) collective-permute-start(f32[8,1152]{1,0:T(8,128)S(1)} %add.12), channel_id=1, source_target_pairs={{0,6},{1,2},{2,1},{3,5},{4,7},{5,3},{6,0},{7,4},{8,11},{9,15},{10,... | collective-permute-start | bytes 110600 | tf_op jit(solution)/shard_map/ppermute | solution.py:223
  7.5 3.4 %collective-permute-start.2 = (f32[8,1152]{1,0:T(8,128)S(1)}, f32[8,1152]{1,0:T(8,128)S(1)}, u32[]{:S(2)}, u32[]{:S(2)}) collective-permute-start(f32[8,1152]{1,0:T(8,128)S(1)} %add.12), channel_id=1, source_target_pairs={{0,5},{1,7},{2,4},{3,6},{4,2},{5,0},{6,3},{7,1},{8,14},{9,12},{10,... | collective-permute-start | bytes 110600 | tf_op jit(solution)/shard_map/ppermute | solution.py:223
  7.5 3.4 %collective-permute-start.3 = (f32[8,1152]{1,0:T(8,128)S(1)}, f32[8,1152]{1,0:T(8,128)S(1)}, u32[]{:S(2)}, u32[]{:S(2)}) collective-permute-start(f32[8,1152]{1,0:T(8,128)S(1)} %add.12), channel_id=1, source_target_pairs={{0,3},{1,4},{2,7},{3,0},{4,1},{5,6},{6,5},{7,2},{8,13},{9,10},{10,... | collective-permute-start | bytes 110600 | tf_op jit(solution)/shard_map/ppermute | solution.py:223
  10.9 4.5 %collective-permute-start.4 = (f32[8,1152]{1,0:T(8,128)S(1)}, f32[8,1152]{1,0:T(8,128)S(1)}, u32[]{:S(2)}, u32[]{:S(2)}) collective-permute-start(f32[8,1152]{1,0:T(8,128)S(1)} %add_add_fusion.held_ref), channel_id=1, source_target_pairs={{0,9},{1,8},{2,11},{3,10},{4,13},{5,12},{6,15},{7,14},{8,1},{9,0},... | collective-permute-start | bytes 110600 | tf_op jit(solution)/shard_map/ppermute | solution.py:223
  15.5 1.2 %collective-permute-start.5 = (bf16[8,1024]{1,0:T(8,128)(2,1)S(1)}, bf16[8,1024]{1,0:T(8,128)(2,1)S(1)}, u32[]{:S(2)}, u32[]{:S(2)}) collective-permute-start(bf16[8,1024]{1,0:T(8,128)(2,1)S(1)} %cube.1.weights_ref), channel_id=1, source_target_pairs={{0,1},{1,0},{2,3},{3,2},{4,5},{5,4},{6,7},{7,6},{8,9},{9,8},{10,11... | collective-permute-start | bytes 49160 | tf_op jit(solution)/shard_map/ppermute | solution.py:223
